TPU v7x, 256 devices: a whole 4x4x8 slice. The times are simulated.
256 devices in a mesh: dp: 4 (over y), brick: 64 (over z, x, core).
Axes of the slice: x: 4, y: 4, z: 8, core: 2. Of those that a mesh axis runs over, the one named last changes fastest.
Arguments:
- features: bfloat16 [4, 512, 512, 64], P('dp', 'brick'), may hold values from -6 to 6
- occupancy: int32 [4, 512, 512], P('dp', 'brick'), may hold values 0 or 1
- neighbours: int32 [4, 512, 27], P('dp', 'brick'), may hold values from -1 to 511, as said below
- owners: int32 [4, 512], P('dp', 'brick'), may hold values from 0 to 511, as said below
- w_conv: bfloat16 [3, 3, 3, 64, 64], replicated, may hold values from -0.15625 to 0.15625
- w_down: bfloat16 [2, 2, 2, 64, 128], replicated, may hold values from -0.25 to 0.25
- w_point: bfloat16 [128, 256], replicated, may hold values from -0.5 to 0.5
- cotangent: bfloat16 [4, 512, 64, 256], P('dp', 'brick'), may hold values from -0.015625 to 0.015625
Outputs:
- grad_w_conv: float32 [3, 3, 3, 64, 64], replicated
- grad_w_down: float32 [2, 2, 2, 64, 128], replicated
- grad_w_point: float32 [128, 256], replicated
Inputs may be any that keep to these rules, and one draw needn't show every extreme that they name: `neighbours`: bricks of a scene form a lattice of 128 x 4 x 1 bricks, 8 consecutive ids a device; an entry names the lattice neighbour at its column's offset or is -1; column 13 is the brick itself. Columns with first offset 0 name bricks of the same device, offset -1 of the same or the previous device, offset +1 of the same or the next. `owners`: within a scene a permutation of the coarse slots; a slot's device is slot // 8. A device hands exactly 1 bricks to each device it hands any to.
All inputs are finite; a program needn't handle non-finite values. No bound on the sum of `occupancy` on one device may be relied on, other than what follows from the above.
Results may differ from a plain program's by a relative error of at most 0.012.
Values may be sent and summed in bfloat16 or wider, within the bound.
A program may use at most 64 MiB of HBM per device.

v0:
```python
import jax
import jax.numpy as jnp
from jax import lax
from jax.sharding import PartitionSpec as P

SPANS = ((7, 8), (0, 8), (0, 1))


def extended(shard, sides, width):
    for axis, dim in sides:
        peers, length = (lax.axis_size(axis), shard.shape[dim])
        up = [(i, (i + 1) % peers) for i in range(peers - 1)]
        down = [(j, i) for i, j in up]
        last = lax.slice_in_dim(shard, length - width, length, axis=dim)
        initial = lax.slice_in_dim(shard, 0, width, axis=dim)
        before = lax.ppermute(last, axis, up)
        after = lax.ppermute(initial, axis, down)
        shard = jnp.concatenate([before, shard, after], axis=dim)
    return shard


def assemble(pools, indices):
    planes = []
    for a in range(3):
        row_parts = []
        for b in range(3):
            col_parts = []
            for c in range(3):
                window_part = pools[a][
                    :, :, SPANS[b][0] : SPANS[b][1], SPANS[c][0] : SPANS[c][1], :
                ]
                col_parts.append(
                    jnp.take(window_part, indices[a][:, 9 * a + 3 * b + c], axis=0, mode="clip")
                )
            row_parts.append(jnp.concatenate(col_parts, axis=3))
        planes.append(jnp.concatenate(row_parts, axis=2))
    return jnp.concatenate(planes, axis=1)


def silu_slope(signal):
    gate_value = jax.nn.sigmoid(signal)
    return gate_value * (1.0 + signal * (1.0 - gate_value))


def point_layer(rows_in, cot_rows, w_point):
    brick_count = rows_in.shape[0]
    row_block = rows_in.reshape(-1, w_point.shape[0])
    point_act = jnp.dot(row_block, w_point, preferred_element_type=jnp.float32)
    grad_point = (
        cot_rows.reshape(point_act.shape).astype(jnp.float32) * silu_slope(point_act)
    ).astype(jnp.bfloat16)
    grad_weight = lax.dot_general(
        row_block, grad_point, (((0,), (0,)), ((), ())), preferred_element_type=jnp.float32
    )
    grad_rows = lax.dot_general(
        grad_point, w_point, (((1,), (1,)), ((), ())), preferred_element_type=jnp.float32
    )
    return (grad_rows.astype(jnp.bfloat16).reshape(brick_count, -1), grad_weight)


def shards(features, occupancy, neighbours, owners, w_conv, w_down, w_point, cotangent):
    brick_count = features.shape[1]
    in_width = features.shape[3]
    brick_devices = lax.axis_size("brick")
    device_pos = lax.axis_index("brick")
    bricks = features[0].reshape(brick_count, 8, 8, 8, in_width)
    link_table = neighbours[0]
    linked = link_table >= 0
    local_ids = link_table - device_pos * brick_count
    zero_brick = jnp.zeros((1, 8, 8, 8, in_width), bricks.dtype)
    beside_all = extended(bricks, (("brick", 0),), brick_count)
    brick_pool = jnp.concatenate([beside_all, zero_brick], axis=0)
    pool_index = jnp.where(linked, local_ids + brick_count, 3 * brick_count)
    padded = assemble(
        (brick_pool[:, 7:8], brick_pool, brick_pool[:, 0:1]), (pool_index, pool_index, pool_index)
    )
    pre_act = lax.conv_general_dilated(
        padded,
        w_conv,
        (1, 1, 1),
        "VALID",
        dimension_numbers=("NDHWC", "DHWIO", "NDHWC"),
        preferred_element_type=jnp.float32,
    )
    occupied = occupancy[0].reshape(brick_count, 8, 8, 8, 1).astype(jnp.float32)
    hidden = (jax.nn.silu(pre_act) * occupied).astype(jnp.bfloat16)
    grouped = hidden.reshape(brick_count, 4, 2, 4, 2, 4, 2, in_width)
    down_act = jnp.einsum(
        "bpiqjrkc,ijkcd->bpqrd", grouped, w_down, preferred_element_type=jnp.float32
    )
    coarse = jax.nn.silu(down_act).astype(jnp.bfloat16).reshape(brick_count, -1)
    target_dev = owners[0] // brick_count
    recv_slot = owners[0] % brick_count
    capacity = max(1, brick_count // brick_devices)
    dest_hits = (target_dev[:, None] == jnp.arange(brick_devices, dtype=jnp.int32)[None, :]).astype(
        jnp.int32
    )
    earlier_hits = jnp.cumsum(dest_hits, axis=0) - dest_hits
    rank_in = jnp.sum(earlier_hits * dest_hits, axis=1)
    position = target_dev * capacity + rank_in
    slot_out = jnp.full((brick_devices * capacity,), -1, jnp.int32).at[position].set(recv_slot)
    arrived = lax.all_to_all(slot_out, "brick", split_axis=0, concat_axis=0, tiled=True)
    present = arrived >= 0
    safe_slots = jnp.where(present, arrived, 0)
    send_rows = (
        jnp.zeros((brick_devices * capacity, coarse.shape[1]), jnp.bfloat16)
        .at[position]
        .set(coarse)
    )
    landed = lax.all_to_all(send_rows, "brick", split_axis=0, concat_axis=0, tiled=True)
    drop_slots = jnp.where(present, arrived, brick_count)
    placed = jnp.zeros_like(coarse).at[drop_slots].set(landed, mode="drop")
    grad_placed, grad_w_point = point_layer(placed, cotangent[0], w_point)
    reply = jnp.where(
        present[:, None], jnp.take(grad_placed, safe_slots, axis=0), jnp.zeros((), jnp.bfloat16)
    )
    returned = lax.all_to_all(reply, "brick", split_axis=0, concat_axis=0, tiled=True)
    grad_coarse = jnp.take(returned, position, axis=0)
    grad_down = (
        grad_coarse.reshape(down_act.shape).astype(jnp.float32) * silu_slope(down_act)
    ).astype(jnp.bfloat16)
    grad_w_down = jnp.einsum(
        "bpiqjrkc,bpqrd->ijkcd", grouped, grad_down, preferred_element_type=jnp.float32
    )
    grad_hidden = jnp.einsum(
        "bpqrd,ijkcd->bpiqjrkc", grad_down, w_down, preferred_element_type=jnp.float32
    )
    grad_hidden = grad_hidden.reshape(brick_count, 8, 8, 8, in_width)
    grad_pre = (grad_hidden * occupied * silu_slope(pre_act)).astype(jnp.bfloat16)
    flat_grad = grad_pre.reshape(-1, in_width)
    term_list = []
    for a in range(3):
        for b in range(3):
            for c in range(3):
                window_part = padded[:, a : a + 8, b : b + 8, c : c + 8, :].reshape(-1, in_width)
                term_list.append(
                    lax.dot_general(
                        window_part,
                        flat_grad,
                        (((0,), (0,)), ((), ())),
                        preferred_element_type=jnp.float32,
                    )
                )
    grad_w_conv = jnp.stack(term_list).reshape(3, 3, 3, in_width, in_width)
    summed = lax.psum((grad_w_conv, grad_w_down, grad_w_point), ("dp", "brick"))
    return (summed[0], summed[1], summed[2])


def solution(mesh):
    in_specs = (
        P("dp", "brick", None, None),
        P("dp", "brick", None),
        P("dp", "brick", None),
        P("dp", "brick"),
        P(),
        P(),
        P(),
        P("dp", "brick", None, None),
    )
    out_specs = (P(), P(), P())
    return jax.shard_map(shards, mesh=mesh, in_specs=in_specs, out_specs=out_specs, check_vma=False)
```

profile of v0, /device:TPU:1, one launch (start us, length us, event | category | flops | bytes accessed | tf_op | source)
XLA Modules:
  0.0 516.5 jit_solution(3569445359638503586)
XLA Ops:
  7.2 1.9 copy.274
  9.1 4.5 collective-permute-start
  13.6 2.0 collective-permute-start.1
  18.5 12.9 %all-to-all-start = ((s32[64,1,1]{2,1,0:T(1,128)}), s32[64,1,1]{2,1,0:T(1,128)S(1)}, u32[]{:S(2)}, u32[]{:S(2)}) async-start(s32[64,1,1]{2,1,0:T(1,128)} %copy.303), calls=%async_computation | async-start | bytes 65536 | tf_op jit(solution)/shard_map/all_to_all | solution.py:102
  42.4 1.2 reduce.18
  44.8 2.9 maximum_maximum_fusion
  50.7 3.0 copy.293
  53.7 0.9 copy.294
  54.6 1.6 gather_fusion.14
  56.3 0.9 copy.291
  57.2 1.6 gather_fusion.12
  77.8 2.8 gather_fusion.13
  80.7 1.2 copy.296
  82.6 2.1 gather_fusion.7
  84.6 1.3 copy.422
  86.0 1.5 copy.281
  87.4 2.1 gather_fusion.5
  89.5 1.3 copy.423
  90.8 1.5 copy.277
  92.3 2.1 gather_fusion.3
  94.4 1.3 copy.424
  96.4 1.5 gather_fusion.1
  97.9 0.9 copy.279
  98.8 1.7 gather_fusion.4
  100.6 1.4 gather_fusion.8
  102.0 1.4 gather_fusion.18
  103.4 1.4 gather_fusion.20
  104.8 1.4 gather_fusion.24
  106.2 1.4 gather_fusion.26
  107.6 1.4 gather_fusion.6
  109.0 1.4 gather_fusion.2
  110.4 1.4 gather_fusion
  111.8 6.8 %multiply_convert_fusion.1 = (bf16[8,8,8,8,64]{4,0,3,2,1:T(8,128)(2,1)S(1)}, f32[8,8,8,8,64]{4,0,3,2,1:T(8,128)}) fusion(f32[8,8,8,8]{0,3,2,1:T(8,128)} %bitcast.539, bf16[3,3,3,64,64]{4,3,2,1,0:T(8,128)(2,1)S(1)} %copy-done, bf16[8,1,1,1,64]{4,0,3,2,1:T(8,128)(2,1)S(1)} %bitcast.601, bf16[8,1,1,8,64]{4,0,3,2,1:T(8,128)(2,1)} %bitcast.573, ...), kind=kOutput, calls=%fused_computation.34 | convolution fusion | flops 920854528 | bytes 2834432 | tf_op jit(solution)/shard_map/conv_general_dilated | solution.py:77
  119.7 1.5 scatter_custom_fusion.1
  121.8 2.1 reduce.56
  123.9 2.6 reshape.781
  126.5 10.3 %all-to-all-start.1 = ((bf16[64,2,4096]{2,1,0:T(2,128)(2,1)}), bf16[64,2,4096]{2,1,0:T(2,128)(2,1)S(1)}, u32[]{:S(2)}, u32[]{:S(2)}) async-start(bf16[64,2,4096]{2,1,0:T(2,128)(2,1)} %reshape.781), calls=%async_computation.1 | async-start | bytes 2097152 | tf_op jit(solution)/shard_map/all_to_all | solution.py:110
  136.8 28.1 %all-to-all-done.1 = bf16[64,2,4096]{2,1,0:T(2,128)(2,1)S(1)} async-done(((bf16[64,2,4096]{2,1,0:T(2,128)(2,1)}), bf16[64,2,4096]{2,1,0:T(2,128)(2,1)S(1)}, u32[]{:S(2)}, u32[]{:S(2)}) %all-to-all-start.1) | async-done | bytes 1048608 | tf_op jit(solution)/shard_map/all_to_all | solution.py:110
  165.0 3.5 reshape.782
  168.5 4.0 scatter_custom_fusion.2
  173.2 1.3 fusion.92
  174.8 1.3 gather_fusion.27
  176.2 1.2 fusion.86
  177.3 2.7 reduce.57
  180.1 1.6 reshape.783
  181.7 6.3 %all-to-all-start.2 = ((bf16[64,2,4096]{2,1,0:T(2,128)(2,1)}), bf16[64,2,4096]{2,1,0:T(2,128)(2,1)S(1)}, u32[]{:S(2)}, u32[]{:S(2)}) async-start(bf16[64,2,4096]{2,1,0:T(2,128)(2,1)} %reshape.783), calls=%async_computation.2 | async-start | bytes 2097152 | tf_op jit(solution)/shard_map/all_to_all | solution.py:117
  188.0 1.3 pad_clamp_fusion
  189.2 1.2 compare_and_fusion.1
  190.5 0.9 copy.319
  191.5 0.9 copy.322
  192.4 6.2 %maximum_maximum_fusion.2 = bf16[8,9,10,10,64]{4,0,3,2,1:T(8,128)(2,1)} fusion(bf16[8,1,1,1,64]{4,0,3,2,1:T(8,128)(2,1)} %bitcast.602, bf16[8,1,1,8,64]{4,0,3,2,1:T(8,128)(2,1)S(1)} %bitcast.574, bf16[8,1,1,1,64]{4,0,3,2,1:T(8,128)(2,1)} %bitcast.598, bf16[8,1,8,1,64]{4,0,3,2,1:T(8,128)(2,1)S(1)} %bitcast.576, bf16[8,1,8,8,64]{4,0,3,2,1:T(8,128)(2,1)S(1)} %bitcast.545, ...), kind=kLoop, calls=%fused_computation.91 | loop fusion | flops 7833600 | bytes 1843200 | tf_op jit(solution)/shard_map/concatenate | solution.py:37
  198.7 3.3 maximum_maximum_fusion.1
  202.9 13.2 %all-to-all-done.2 = bf16[64,2,4096]{2,1,0:T(2,128)(2,1)S(1)} async-done(((bf16[64,2,4096]{2,1,0:T(2,128)(2,1)}), bf16[64,2,4096]{2,1,0:T(2,128)(2,1)S(1)}, u32[]{:S(2)}, u32[]{:S(2)}) %all-to-all-start.2) | async-done | bytes 1048608 | tf_op jit(solution)/shard_map/all_to_all | solution.py:117
  216.1 3.5 reshape.784
  219.6 2.8 copy.406
  223.2 1.8 convolution_bitcast_fusion.1
  226.5 1.3 copy-done.3
  227.8 1.1 multiply_convert_fusion
  238.1 1.0 fusion.72
  240.6 1.0 copy-done.4
  246.3 0.9 copy-done.12
  247.3 257.7 %all-reduce.3.cloned.1.call-done = (f32[3,3,3,64,64]{4,3,2,1,0:T(8,128)}, f32[2,2,2,64,128]{4,3,0,1,2:T(8,128)}, f32[128,256]{1,0:T(8,128)}) async-done(((f32[3,3,3,64,64]{4,3,2,1,0:T(8,128)}, f32[2,2,2,64,128]{4,3,0,1,2:T(8,128)}, f32[128,256]{1,0:T(8,128)}), (f32[3,3,3,64,64]{4,3,2,1,0:T(8,128)}, f32[2,2,2,64,128]{4,3,0,1,2:T(8,128)}, f32[128,256]{1,0:T(8,128)})) %all-reduce.3.cloned.1.call-update) | async-done | bytes 835600 | tf_op jit(solution)/shard_map/psum | solution.py:145
  504.9 1.7 copy.325
  506.6 2.2 copy.457
  (224 shorter events, 60.4 us)
Async XLA Ops:
  7.2 104.6 %copy-start = (bf16[3,3,3,64,64]{4,3,2,1,0:T(8,128)(2,1)S(1)}, bf16[3,3,3,64,64]{4,3,2,1,0:T(8,128)(2,1)}, u32[]{:S(2)}) copy-start(bf16[3,3,3,64,64]{4,3,2,1,0:T(8,128)(2,1)} %param.12) | copy-start | bytes 663556
  9.1 35.7 %collective-permute-start = (bf16[8,8,8,8,64]{4,0,3,2,1:T(8,128)(2,1)S(1)}, bf16[8,8,8,8,64]{4,0,3,2,1:T(8,128)(2,1)S(1)}, u32[]{:S(2)}, u32[]{:S(2)}) collective-permute-start(bf16[8,8,8,8,64]{4,0,3,2,1:T(8,128)(2,1)S(1)} %bitcast.503), channel_id=1, source_target_pairs={{0,1},{1,2},{2,3},{3,4},{4,5},{5,6},{6,7},{7,8},{8,9},{9,10},{10,1... | collective-permute-start | bytes 1572872 | tf_op jit(solution)/shard_map/ppermute | solution.py:16
  13.6 31.2 %collective-permute-start.1 = (bf16[8,8,8,8,64]{4,0,3,2,1:T(8,128)(2,1)S(1)}, bf16[8,8,8,8,64]{4,0,3,2,1:T(8,128)(2,1)}, u32[]{:S(2)}, u32[]{:S(2)}) collective-permute-start(bf16[8,8,8,8,64]{4,0,3,2,1:T(8,128)(2,1)S(1)} %bitcast.504), channel_id=1, source_target_pairs={{1,0},{2,1},{3,2},{4,3},{5,4},{6,5},{7,6},{8,7},{9,8},{10,9},{11,1... | collective-permute-start | bytes 1572872 | tf_op jit(solution)/shard_map/ppermute | solution.py:17
  16.2 2.3 copy-start.47
  16.5 2.0 copy-start.50
  17.2 1.3 copy-start.51
  18.5 23.9 %all-to-all-start = ((s32[64,1,1]{2,1,0:T(1,128)}), s32[64,1,1]{2,1,0:T(1,128)S(1)}, u32[]{:S(2)}, u32[]{:S(2)}) async-start(s32[64,1,1]{2,1,0:T(1,128)} %copy.303), calls=%async_computation | async-start | bytes 65536 | tf_op jit(solution)/shard_map/all_to_all | solution.py:102
  43.6 4.1 copy-start.48
  60.3 14.6 %copy-start.21 = (bf16[25,8,64]{2,0,1:T(8,128)(2,1)S(1)}, bf16[25,8,64]{2,0,1:T(8,128)(2,1)}, u32[]{:S(2)}) copy-start(bf16[25,8,64]{2,0,1:T(8,128)(2,1)} %get-tuple-element.47) | copy-start | bytes 76804
  66.8 44.9 %copy-start.6 = (bf16[8,8,8,64]{3,0,2,1:T(8,128)(2,1)}, bf16[8,8,8,64]{3,0,2,1:T(8,128)(2,1)S(1)}, u32[]{:S(2)}) copy-start(bf16[8,8,8,64]{3,0,2,1:T(8,128)(2,1)S(1)} %copy.409) | copy-start | bytes 196612
  80.6 20.0 %copy-start.1 = (bf16[8,8,8,8,64]{4,3,2,1,0:T(8,128)(2,1)}, bf16[8,8,8,8,64]{4,3,2,1,0:T(8,128)(2,1)S(1)}, u32[]{:S(2)}) copy-start(bf16[8,8,8,8,64]{4,3,2,1,0:T(8,128)(2,1)S(1)} %gather_fusion.13) | copy-start | bytes 1572868
  80.6 1.3 copy-start.20
  97.9 20.7 %copy-start.32 = (bf16[8,8,64]{2,0,1:T(8,128)(2,1)}, bf16[8,8,64]{2,0,1:T(8,128)(2,1)S(1)}, u32[]{:S(2)}) copy-start(bf16[8,8,64]{2,0,1:T(8,128)(2,1)S(1)} %copy.425) | copy-start | bytes 24580
  100.6 18.0 %copy-start.14 = (bf16[8,8,8,64]{3,0,2,1:T(8,128)(2,1)}, bf16[8,8,8,64]{3,0,2,1:T(8,128)(2,1)S(1)}, u32[]{:S(2)}) copy-start(bf16[8,8,8,64]{3,0,2,1:T(8,128)(2,1)S(1)} %copy.413) | copy-start | bytes 196612
  102.0 16.6 %copy-start.35 = (bf16[8,64]{1,0:T(8,128)(2,1)}, bf16[8,64]{1,0:T(8,128)(2,1)S(1)}, u32[]{:S(2)}) copy-start(bf16[8,64]{1,0:T(8,128)(2,1)S(1)} %gather_fusion.8) | copy-start | bytes 3076
  103.4 15.2 %copy-start.37 = (bf16[8,64]{1,0:T(8,128)(2,1)}, bf16[8,64]{1,0:T(8,128)(2,1)S(1)}, u32[]{:S(2)}) copy-start(bf16[8,64]{1,0:T(8,128)(2,1)S(1)} %gather_fusion.18) | copy-start | bytes 3076
  104.8 13.8 %copy-start.38 = (bf16[8,64]{1,0:T(8,128)(2,1)}, bf16[8,64]{1,0:T(8,128)(2,1)S(1)}, u32[]{:S(2)}) copy-start(bf16[8,64]{1,0:T(8,128)(2,1)S(1)} %gather_fusion.20) | copy-start | bytes 3076
  106.2 12.4 %copy-start.41 = (bf16[8,64]{1,0:T(8,128)(2,1)}, bf16[8,64]{1,0:T(8,128)(2,1)S(1)}, u32[]{:S(2)}) copy-start(bf16[8,64]{1,0:T(8,128)(2,1)S(1)} %gather_fusion.24) | copy-start | bytes 3076
  107.6 11.0 %copy-start.44 = (bf16[8,64]{1,0:T(8,128)(2,1)}, bf16[8,64]{1,0:T(8,128)(2,1)S(1)}, u32[]{:S(2)}) copy-start(bf16[8,64]{1,0:T(8,128)(2,1)S(1)} %gather_fusion.26) | copy-start | bytes 3076
  109.0 9.6 %copy-start.39 = (bf16[8,64]{1,0:T(8,128)(2,1)}, bf16[8,64]{1,0:T(8,128)(2,1)S(1)}, u32[]{:S(2)}) copy-start(bf16[8,64]{1,0:T(8,128)(2,1)S(1)} %gather_fusion.6) | copy-start | bytes 3076
  110.4 8.3 %copy-start.42 = (bf16[8,64]{1,0:T(8,128)(2,1)}, bf16[8,64]{1,0:T(8,128)(2,1)S(1)}, u32[]{:S(2)}) copy-start(bf16[8,64]{1,0:T(8,128)(2,1)S(1)} %gather_fusion.2) | copy-start | bytes 3076
  111.8 6.9 %copy-start.45 = (bf16[8,64]{1,0:T(8,128)(2,1)}, bf16[8,64]{1,0:T(8,128)(2,1)S(1)}, u32[]{:S(2)}) copy-start(bf16[8,64]{1,0:T(8,128)(2,1)S(1)} %gather_fusion) | copy-start | bytes 3076
  111.8 6.9 %copy-start.24 = (bf16[2,2,2,64,128]{4,3,2,1,0:T(8,128)(2,1)S(1)}, bf16[2,2,2,64,128]{4,3,2,1,0:T(8,128)(2,1)}, u32[]{:S(2)}) copy-start(bf16[2,2,2,64,128]{4,3,2,1,0:T(8,128)(2,1)} %param.13) | copy-start | bytes 393220
  118.6 1.0 copy-start.53
  119.0 0.7 copy-start.9
  123.9 12.9 %copy-start.49 = (s32[64]{0:T(128)S(1)}, s32[64]{0:T(128)}, u32[]{:S(2)}) copy-start(s32[64]{0:T(128)} %copy-done.48) | copy-start | bytes 772
  126.5 38.5 %all-to-all-start.1 = ((bf16[64,2,4096]{2,1,0:T(2,128)(2,1)}), bf16[64,2,4096]{2,1,0:T(2,128)(2,1)S(1)}, u32[]{:S(2)}, u32[]{:S(2)}) async-start(bf16[64,2,4096]{2,1,0:T(2,128)(2,1)} %reshape.781), calls=%async_computation.1 | async-start | bytes 2097152 | tf_op jit(solution)/shard_map/all_to_all | solution.py:110
  136.8 36.4 %copy-start.34 = (bf16[128,256]{1,0:T(8,128)(2,1)S(1)}, bf16[128,256]{1,0:T(8,128)(2,1)}, u32[]{:S(2)}) copy-start(bf16[128,256]{1,0:T(8,128)(2,1)} %param.14) | copy-start | bytes 196612
  172.6 0.6 copy-start.16
  180.0 12.4 %copy-start.7 = (bf16[8,8,8,64]{3,0,2,1:T(8,128)(2,1)S(1)}, bf16[8,8,8,64]{3,0,2,1:T(8,128)(2,1)}, u32[]{:S(2)}) copy-start(bf16[8,8,8,64]{3,0,2,1:T(8,128)(2,1)} %copy-done.6) | copy-start | bytes 196612
  180.0 12.4 %copy-start.8 = (bf16[8,8,8,64]{3,0,2,1:T(8,128)(2,1)S(1)}, bf16[8,8,8,64]{3,0,2,1:T(8,128)(2,1)}, u32[]{:S(2)}) copy-start(bf16[8,8,8,64]{3,0,2,1:T(8,128)(2,1)} %copy.412) | copy-start | bytes 196612
  180.0 12.4 %copy-start.13 = (bf16[8,8,8,64]{3,0,2,1:T(8,128)(2,1)S(1)}, bf16[8,8,8,64]{3,0,2,1:T(8,128)(2,1)}, u32[]{:S(2)}) copy-start(bf16[8,8,8,64]{3,0,2,1:T(8,128)(2,1)} %copy.408) | copy-start | bytes 196612
  180.0 12.4 %copy-start.22 = (bf16[8,8,64]{2,0,1:T(8,128)(2,1)S(1)}, bf16[8,8,64]{2,0,1:T(8,128)(2,1)}, u32[]{:S(2)}) copy-start(bf16[8,8,64]{2,0,1:T(8,128)(2,1)} %copy.420) | copy-start | bytes 24580
  180.0 12.4 %copy-start.23 = (bf16[8,8,64]{2,0,1:T(8,128)(2,1)S(1)}, bf16[8,8,64]{2,0,1:T(8,128)(2,1)}, u32[]{:S(2)}) copy-start(bf16[8,8,64]{2,0,1:T(8,128)(2,1)} %copy.421) | copy-start | bytes 24580
  180.0 12.4 %copy-start.27 = (bf16[8,8,64]{2,0,1:T(8,128)(2,1)S(1)}, bf16[8,8,64]{2,0,1:T(8,128)(2,1)}, u32[]{:S(2)}) copy-start(bf16[8,8,64]{2,0,1:T(8,128)(2,1)} %copy.414) | copy-start | bytes 24580
  180.1 12.4 %copy-start.28 = (bf16[8,8,64]{2,0,1:T(8,128)(2,1)S(1)}, bf16[8,8,64]{2,0,1:T(8,128)(2,1)}, u32[]{:S(2)}) copy-start(bf16[8,8,64]{2,0,1:T(8,128)(2,1)} %copy.415) | copy-start | bytes 24580
  181.7 34.5 %all-to-all-start.2 = ((bf16[64,2,4096]{2,1,0:T(2,128)(2,1)}), bf16[64,2,4096]{2,1,0:T(2,128)(2,1)S(1)}, u32[]{:S(2)}, u32[]{:S(2)}) async-start(bf16[64,2,4096]{2,1,0:T(2,128)(2,1)} %reshape.783), calls=%async_computation.2 | async-start | bytes 2097152 | tf_op jit(solution)/shard_map/all_to_all | solution.py:117
  187.9 317.0 %all-reduce.3.cloned.1.call-start = ((), (), s32[]{:S(2)}) async-start(), calls=%async_computation.3 | async-start | bytes 2555904 | tf_op jit(solution)/shard_map/psum | solution.py:145
  191.4 7.2 %copy-start.15 = (bf16[8,8,8,64]{3,0,2,1:T(8,128)(2,1)S(1)}, bf16[8,8,8,64]{3,0,2,1:T(8,128)(2,1)}, u32[]{:S(2)}) copy-start(bf16[8,8,8,64]{3,0,2,1:T(8,128)(2,1)} %copy-done.14) | copy-start | bytes 196612
  191.4 7.2 %copy-start.29 = (bf16[8,8,64]{2,0,1:T(8,128)(2,1)S(1)}, bf16[8,8,64]{2,0,1:T(8,128)(2,1)}, u32[]{:S(2)}) copy-start(bf16[8,8,64]{2,0,1:T(8,128)(2,1)} %copy.422) | copy-start | bytes 24580
  191.4 7.2 %copy-start.30 = (bf16[8,8,64]{2,0,1:T(8,128)(2,1)S(1)}, bf16[8,8,64]{2,0,1:T(8,128)(2,1)}, u32[]{:S(2)}) copy-start(bf16[8,8,64]{2,0,1:T(8,128)(2,1)} %copy.423) | copy-start | bytes 24580
  191.4 7.2 %copy-start.31 = (bf16[8,8,64]{2,0,1:T(8,128)(2,1)S(1)}, bf16[8,8,64]{2,0,1:T(8,128)(2,1)}, u32[]{:S(2)}) copy-start(bf16[8,8,64]{2,0,1:T(8,128)(2,1)} %copy.424) | copy-start | bytes 24580
  191.4 7.2 %copy-start.33 = (bf16[8,8,64]{2,0,1:T(8,128)(2,1)S(1)}, bf16[8,8,64]{2,0,1:T(8,128)(2,1)}, u32[]{:S(2)}) copy-start(bf16[8,8,64]{2,0,1:T(8,128)(2,1)} %copy-done.32) | copy-start | bytes 24580
  191.4 7.2 %copy-start.36 = (bf16[8,64]{1,0:T(8,128)(2,1)S(1)}, bf16[8,64]{1,0:T(8,128)(2,1)}, u32[]{:S(2)}) copy-start(bf16[8,64]{1,0:T(8,128)(2,1)} %copy-done.35) | copy-start | bytes 3076
  191.4 7.2 %copy-start.40 = (bf16[8,64]{1,0:T(8,128)(2,1)S(1)}, bf16[8,64]{1,0:T(8,128)(2,1)}, u32[]{:S(2)}) copy-start(bf16[8,64]{1,0:T(8,128)(2,1)} %copy-done.39) | copy-start | bytes 3076
  191.4 7.2 %copy-start.43 = (bf16[8,64]{1,0:T(8,128)(2,1)S(1)}, bf16[8,64]{1,0:T(8,128)(2,1)}, u32[]{:S(2)}) copy-start(bf16[8,64]{1,0:T(8,128)(2,1)} %copy-done.42) | copy-start | bytes 3076
  191.5 7.2 %copy-start.46 = (bf16[8,64]{1,0:T(8,128)(2,1)S(1)}, bf16[8,64]{1,0:T(8,128)(2,1)}, u32[]{:S(2)}) copy-start(bf16[8,64]{1,0:T(8,128)(2,1)} %copy-done.45) | copy-start | bytes 3076
  198.7 3.3 copy-start.17
  219.6 3.5 copy-start.10
  219.6 3.5 copy-start.52
  223.2 1.8 copy-start.25
  226.2 1.6 copy-start.3
  226.2 1.6 copy-start.11
  227.8 1.5 copy-start.5
  234.9 1.2 copy-start.2
  234.9 1.3 copy-start.19
  237.1 1.0 copy-start.18
  240.1 1.5 copy-start.4
  246.3 0.9 copy-start.12
  504.9 3.9 copy-start.26
Sparse Core Ops, SparseCore 0:
  247.4 257.5 all-reduce.2
where the time goes:
time: 523 us; the launch traced here: 517 us
  waiting for transfers between devices  299 us (57%)
  local copies, waits for them, and re-layouts  104 us (20%)
  starting transfers between devices  36 us (7%)
  other arithmetic  35.2 us (7%)
  matrix products  26.6 us (5%)
  between operations  15.2 us (3%)
    psum x1, waiting for transfers between devices, shards(): summed = lax.psum((grad_w_conv, grad_w_down, grad_w_point), ('dp', 'brick'))  258 us
    gather x48, local copies, waits for them, and re-layouts, assemble(): jnp.take(window_part, indices[a][:, 9 * a + 3 * b + c], axis=0, mode='clip')  46 us
    all_to_all x1, waiting for transfers between devices, shards(): lax.all_to_all(send_rows, 'brick', split_axis=0, concat_axis=0, tiled=True)  28.1 us
    unnamed x117, local copies, waits for them, and re-layouts  26.5 us
    slice x22, local copies, waits for them, and re-layouts, assemble(): pools[a][:, :, SPANS[b][0]:SPANS[b][1], SPANS[c][0]:SPANS[c][1], :]  15.4 us
    dot_general x27, matrix products, shards(): lax.dot_general(window_part, flat_grad, (((0,), (0,)), ((), ())), preferr...  14.9 us
    all_to_all x1, waiting for transfers between devices, shards(): lax.all_to_all(reply, 'brick', split_axis=0, concat_axis=0, tiled=True)  13.2 us
    all_to_all x1, starting transfers between devices, shards(): lax.all_to_all(slot_out, 'brick', split_axis=0, concat_axis=0, tiled=True)  12.9 us
  transfers between devices with their start and end apart: 6, of which 3 were waited for; matrix products, arithmetic and copies ran while one was open for 6% of the time, Pallas kernels for 0%

commit v1 on v0

v1 whole, which is shorter than its diff:
```python
import jax
import jax.numpy as jnp
import numpy as np
from jax import lax
from jax.experimental import pallas as pl
from jax.experimental.pallas import tpu as pltpu
from jax.sharding import PartitionSpec as P

MESH = pl.DeviceIdType.MESH
NX = 4
NC = 2
NSUB = 4
BF = jnp.bfloat16
F32 = jnp.float32


def where_am_i():
    spot = lax.axis_index("brick")
    return spot // (NX * NC), spot // NC % NX, spot % NC


def brick_at(z, x, c):
    return (z * NX + x) * NC + c


def greet(mates):
    barrier = pltpu.get_barrier_semaphore()
    for mate in mates:
        pl.semaphore_signal(barrier, inc=1, device_id=mate, device_id_type=MESH)
    pl.semaphore_wait(barrier, len(mates))


def exchange_kernel(
    nz, up_ref, down_ref, cot_ref, dec_ref, before_ref, after_ref, out_ref,
    before_in, after_in, pool0, pool1, pool2, pool3, picked, landed, dec_in, dec_s,
    halo_send, halo_recv, dec_send, dec_recv, dec_sem,
    right_send, right_recv, left_send, left_recv, pair_send, pair_recv, row_send, row_recv,
):
    z, x, c = where_am_i()
    spot = lax.axis_index("brick")
    total = nz * NX * NC
    zr, zl = (z + 1) % nz, (z + nz - 1) % nz
    right, left = {"brick": brick_at(zr, x, c)}, {"brick": brick_at(zl, x, c)}
    pair = {"brick": brick_at(z, x, 1 - c)}
    row = [{"brick": brick_at(z, (x + g) % NX, c)} for g in range(1, NX)]
    ahead, behind = {"brick": (spot + 1) % total}, {"brick": (spot + total - 1) % total}
    greet([right, left, pair, ahead, behind] + row)

    pools = [pool0, pool1, pool2, pool3]
    pending = []

    def send(src, dst, ssem, rsem, mate):
        copy = pltpu.make_async_remote_copy(
            src_ref=src, dst_ref=dst, send_sem=ssem, recv_sem=rsem, device_id=mate, device_id_type=MESH
        )
        copy.start()
        pending.append(copy)
        return copy

    dec_copies = [
        send(dec_ref, dec_in.at[g], dec_send.at[g], dec_recv.at[g], row[g]) for g in range(NX - 1)
    ]
    halo_up = send(up_ref, before_in, halo_send.at[0], halo_recv.at[0], ahead)
    halo_down = send(down_ref, after_in, halo_send.at[1], halo_recv.at[1], behind)

    cells = cot_ref.shape[1] // NSUB

    def own(k):
        return cot_ref.at[:, pl.ds(k * cells, cells), :]

    far = nz // 2
    rights, lefts, pairs, rows = {}, {}, {}, {}

    def start_own(k):
        rights[1, k] = send(own(k), pools[k].at[c, z], right_send.at[0, k], right_recv.at[0, k], right)
        lefts[1, k] = send(own(k), pools[k].at[c, z], left_send.at[0, k], left_recv.at[0, k], left)
        pairs[0, k] = send(own(k), pools[k].at[c, z], pair_send.at[0, k], pair_recv.at[0, k], pair)
        pools[k][c, z] = cot_ref[:, k * cells : (k + 1) * cells, :]

    def goes_right(s, k):
        return s < far or (s == far and k % 2 == 0)

    def goes_left(s, k):
        return s < far or (s == far and k % 2 == 1)

    halves = [(0, 1), (2, 3)]
    for k in halves[0]:
        start_own(k)
    for g in range(NX - 1):
        dec_copies[g].wait_recv()
        local = pltpu.make_async_copy(dec_in.at[g], dec_s.at[g], dec_sem.at[g])
        local.start()
        local.wait()
    local = pltpu.make_async_copy(dec_ref, dec_s.at[NX - 1], dec_sem.at[NX - 1])
    local.start()
    local.wait()

    def pick(g, k, b):
        return pools[k][dec_s[g, 0, b], dec_s[g, 1, b], dec_s[g, 2, b]]

    for h, ks in enumerate(halves):
        for s in range(1, far + 1):
            if s == far and h + 1 < len(halves):
                for k in halves[h + 1]:
                    start_own(k)
            for k in ks:
                if goes_right(s, k):
                    rights[s, k].wait_recv()
                    home = pools[k].at[c, (z + nz - s) % nz]
                    if goes_right(s + 1, k):
                        rights[s + 1, k] = send(home, home, right_send.at[s, k], right_recv.at[s, k], right)
                    pairs[s, k] = send(home, home, pair_send.at[s, k], pair_recv.at[s, k], pair)
                if goes_left(s, k):
                    lefts[s, k].wait_recv()
                    home = pools[k].at[c, (z + s) % nz]
                    if goes_left(s + 1, k):
                        lefts[s + 1, k] = send(home, home, left_send.at[s, k], left_recv.at[s, k], left)
                    if s < far:
                        t = nz - s
                        pairs[t, k] = send(home, home, pair_send.at[t, k], pair_recv.at[t, k], pair)
                    else:
                        pairs[s, k] = send(home, home, pair_send.at[s, k], pair_recv.at[s, k], pair)
        for k in ks:
            for t in range(nz):
                pairs[t, k].wait_recv()
            for g in range(NX - 1):
                for b in range(8):
                    picked[g, k, b] = pick(NX - 2 - g, k, b)
                rows[g, k] = send(picked.at[g, k], landed.at[x, k], row_send.at[g, k], row_recv.at[g, k], row[g])
            for b in range(8):
                landed[x, k, b] = pick(NX - 1, k, b)

    halo_up.wait_recv()
    halo_down.wait_recv()
    before_ref[...] = before_in[...]
    after_ref[...] = after_in[...]
    for k in range(NSUB):
        for g in range(NX - 1):
            rows[g, k].wait_recv()
    for b in range(8):
        for k in range(NSUB):
            out_ref[b, k * cells : (k + 1) * cells, :] = landed[dec_s[NX - 1, 3, b], k, b]
    for copy in pending:
        copy.wait_send()


def exchange(nz, up_face, down_face, cot, dec):
    slots, cells, wide = cot.shape
    chunk = (slots, cells // NSUB, wide)
    dma = pltpu.SemaphoreType.DMA
    vmem = pl.BlockSpec(memory_space=pltpu.VMEM)
    far = nz // 2
    return pl.pallas_call(
        lambda *refs: exchange_kernel(nz, *refs),
        out_shape=(
            jax.ShapeDtypeStruct(up_face.shape, BF),
            jax.ShapeDtypeStruct(down_face.shape, BF),
            jax.ShapeDtypeStruct(cot.shape, BF),
        ),
        in_specs=[vmem] * 4,
        out_specs=(vmem,) * 3,
        scratch_shapes=[
            pltpu.VMEM(up_face.shape, BF),
            pltpu.VMEM(down_face.shape, BF),
            *[pltpu.VMEM((NC, nz) + chunk, BF)] * NSUB,
            pltpu.VMEM((NX - 1, NSUB) + chunk, BF),
            pltpu.VMEM((NX, NSUB) + chunk, BF),
            pltpu.VMEM((NX - 1, 8, 128), jnp.int32),
            pltpu.SMEM((NX, 8, 128), jnp.int32),
            dma((2,)), dma((2,)), dma((NX - 1,)), dma((NX - 1,)), dma((NX,)),
            dma((far, NSUB)), dma((far, NSUB)), dma((far, NSUB)), dma((far, NSUB)),
            dma((nz, NSUB)), dma((nz, NSUB)), dma((NX - 1, NSUB)), dma((NX - 1, NSUB)),
        ],
        compiler_params=pltpu.CompilerParams(collective_id=0, has_side_effects=True),
        name="exchange",
    )(up_face, down_face, cot, dec)


def slope_of(v):
    g = 1.0 / (1.0 + jnp.exp(-v))
    return g * (1.0 + v * (1.0 - g))


def silu_of(v):
    return v / (1.0 + jnp.exp(-v))


def dot(a, b, ca=1, cb=0):
    return lax.dot_general(a, b, (((ca,), (cb,)), ((), ())), preferred_element_type=F32)


def compute_kernel(
    src_ref, before_ref, after_ref, tgt_ref, occ_ref, u_ref, wd_ref, wp_ref, cot_ref, part_ref,
    source, taps, pre, hid_t, gpre_t, sums,
):
    source[0:512] = src_ref[...]
    source[512:544] = before_ref[...]
    source[544:576] = after_ref[...]
    pre[...] = jnp.zeros_like(pre)
    tgt = tgt_ref[...]
    which = lax.broadcasted_iota(jnp.int32, tgt.shape, 1)
    spots = lax.broadcasted_iota(jnp.int32, (512, 576), 1).astype(F32)

    def tap_step(tap, carry):
        column = jnp.sum(jnp.where(which == tap, tgt, 0.0), axis=1, keepdims=True)
        pick = jnp.where(spots == column, 1.0, 0.0).astype(BF)
        rows = dot(pick, source[...]).astype(BF)
        taps[tap] = rows
        for t in range(4):
            at = slice(128 * t, 128 * t + 128)
            pre[:, at] += dot(rows[:, 128 * t : 128 * t + 256], u_ref[tap])
        return carry

    lax.fori_loop(0, 9, tap_step, 0)

    spread = (
        lax.broadcasted_iota(jnp.int32, (8, 512), 1) // 64 == lax.broadcasted_iota(jnp.int32, (8, 512), 0)
    ).astype(F32).astype(BF)
    occ = dot(occ_ref[...], spread)
    hidden = (silu_of(pre[...]) * occ).astype(BF)
    for r in range(4):
        for ij in range(4):
            hid_t[128 * r : 128 * r + 128, 128 * ij : 128 * ij + 128] = hidden[
                128 * ij : 128 * ij + 128, 128 * r : 128 * r + 128
            ]
    down = dot(hid_t[...], wd_ref[...])
    coarse = silu_of(down).astype(BF)
    row = lax.broadcasted_iota(jnp.int32, (512, 512), 0)
    col = lax.broadcasted_iota(jnp.int32, (512, 512), 1)
    order = jnp.where(col == 4 * (row % 128) + row // 128, 1.0, 0.0).astype(BF)
    cot = dot(order, cot_ref[...])
    point = dot(coarse, wp_ref[...])
    gpoint = (cot * slope_of(point)).astype(BF)
    gwp = dot(coarse, gpoint, 0, 0)
    gplaced = dot(gpoint, wp_ref[...], 1, 1).astype(BF)
    gdown = (gplaced.astype(F32) * slope_of(down)).astype(BF)
    gwd = dot(hid_t[...], gdown, 0, 0)
    ghid = dot(gdown, wd_ref[...], 1, 1)
    for r in range(4):
        for ij in range(4):
            a = slice(128 * ij, 128 * ij + 128)
            b = slice(128 * r, 128 * r + 128)
            piece = (ghid[b, a] * occ[a, b] * slope_of(pre[a, b])).astype(BF)
            gpre_t[b, a] = piece.T

    def grad_step(tap, carry):
        total = jnp.zeros((128, 256), F32)
        for t in range(4):
            total += dot(gpre_t[128 * t : 128 * t + 128, :], taps[tap, :, 128 * t : 128 * t + 256])
        sums[tap] = total.T
        return carry

    for tap in range(9):
        grad_step(tap, 0)
    low = lax.broadcasted_iota(jnp.int32, (64, 128), 1) < 64

    def block(m):
        tap, c = m // 3, m % 3
        return sums[tap, 64 * c : 64 * c + 64, :], sums[tap, 64 * c + 64 : 64 * c + 128, :]

    for j in range(14):
        a0, a1 = block(2 * j)
        even = a0 + pltpu.roll(a1, 64, 1)
        if 2 * j + 1 < 27:
            b0, b1 = block(2 * j + 1)
            odd = pltpu.roll(b0, 64, 1) + b1
        else:
            odd = jnp.zeros_like(even)
        part_ref[j] = jnp.where(low, even, odd)
    for j in range(8):
        part_ref[14 + j] = gwd[64 * j : 64 * j + 64, :]
    for j in range(4):
        r, t = j % 2, j // 2
        part_ref[22 + j] = gwp[64 * r : 64 * r + 64, 128 * t : 128 * t + 128]
    for j in range(26, 32):
        part_ref[j] = jnp.zeros((64, 128), F32)


def compute(src, before, after, tgt, occ, u, wd, wp, cot):
    vmem = pl.BlockSpec(memory_space=pltpu.VMEM)
    return pl.pallas_call(
        compute_kernel,
        out_shape=jax.ShapeDtypeStruct((32, 64, 128), F32),
        in_specs=[vmem] * 9,
        out_specs=vmem,
        scratch_shapes=[
            pltpu.VMEM((576, 640), BF),
            pltpu.VMEM((9, 512, 640), BF),
            pltpu.VMEM((512, 512), F32),
            pltpu.VMEM((512, 512), BF),
            pltpu.VMEM((512, 512), BF),
            pltpu.VMEM((9, 256, 128), F32),
        ],
        name="compute",
    )(src, before, after, tgt, occ, u, wd, wp, cot)


def reduce_kernel(
    nz, ny, part_ref, gwc_ref, gwd_ref, gwp_ref,
    tosend, arrived, plane_out, plane_in, depth_out, depth_in, full,
    pair_send, pair_recv, plane_send, plane_recv, depth_send, depth_recv,
    back_send, back_recv, share_send, share_recv,
):
    z, x, c = where_am_i()
    y = lax.axis_index("dp")
    np_ = ny * NX
    me = y * NX + x
    pair = {"dp": y, "brick": brick_at(z, x, 1 - c)}
    plane = []
    for g in range(1, np_):
        yy, xx = (y + g // NX) % ny, (x + g % NX) % NX
        plane.append(({"dp": yy, "brick": brick_at(z, xx, c)}, yy * NX + xx, g))
    depth = [{"dp": y, "brick": brick_at((z + g) % nz, x, c)} for g in range(1, nz)]
    greet([pair] + [p[0] for p in plane] + depth)
    pending = []

    def send(src, dst, ssem, rsem, mate):
        copy = pltpu.make_async_remote_copy(
            src_ref=src, dst_ref=dst, send_sem=ssem, recv_sem=rsem, device_id=mate, device_id_type=MESH
        )
        copy.start()
        pending.append(copy)
        return copy

    pieces = 4
    size = np_ // pieces
    firsts = []
    for i in range(pieces):
        tosend[pl.ds(i * size, size)] = part_ref[pl.ds((1 - c) * np_ + i * size, size)].astype(BF)
        at = pl.ds(i * size, size)
        firsts.append(send(tosend.at[at], arrived.at[at], pair_send.at[i], pair_recv.at[i], pair))
    for i in range(pieces):
        firsts[i].wait_recv()
        at = pl.ds(i * size, size)
        plane_out[at] = (part_ref[pl.ds(c * np_ + i * size, size)] + arrived[at].astype(F32)).astype(BF)
    seconds = [
        send(plane_out.at[k], plane_in.at[g], plane_send.at[g], plane_recv.at[g], mate) for mate, k, g in plane
    ]
    total = plane_out[me].astype(F32)
    for g in range(1, np_):
        seconds[g - 1].wait_recv()
        total += plane_in[g].astype(F32)
    depth_out[...] = total.astype(BF)
    thirds = [
        send(depth_out, depth_in.at[z], depth_send.at[g], depth_recv.at[g], mate) for g, mate in enumerate(depth)
    ]
    depth_in[z] = total.astype(BF)
    for copy in thirds:
        copy.wait_recv()
    total = depth_in[0].astype(F32)
    for k in range(1, nz):
        total += depth_in[k].astype(F32)
    mine = full.at[c, me]
    full[c, me] = total.astype(BF)
    backs = [send(mine, mine, back_send.at[g], back_recv.at[g], mate) for mate, k, g in plane]
    shares = [send(mine, mine, share_send.at[0], share_recv.at[0], pair)]
    for g in range(1, np_):
        backs[g - 1].wait_recv()
        yy, xx = (y + ny - g // NX) % ny, (x + NX - g % NX) % NX
        home = full.at[c, yy * NX + xx]
        shares.append(send(home, home, share_send.at[g], share_recv.at[g], pair))
    for copy in shares:
        copy.wait_recv()
    for j in range(14):
        chunk = full[j // np_, j % np_].astype(F32)
        gwc_ref[2 * j] = chunk[:, :64]
        if 2 * j + 1 < 27:
            gwc_ref[2 * j + 1] = pltpu.roll(chunk, 64, 1)[:, :64]
    for j in range(8):
        k = 14 + j
        gwd_ref[64 * j : 64 * j + 64, :] = full[k // np_, k % np_].astype(F32)
    for j in range(4):
        r, t = j % 2, j // 2
        k = 22 + j
        gwp_ref[64 * r : 64 * r + 64, 128 * t : 128 * t + 128] = full[k // np_, k % np_].astype(F32)
    for copy in pending:
        copy.wait_send()


def reduce_all(nz, ny, part):
    vmem = pl.BlockSpec(memory_space=pltpu.VMEM)
    dma = pltpu.SemaphoreType.DMA
    np_ = ny * NX
    return pl.pallas_call(
        lambda *refs: reduce_kernel(nz, ny, *refs),
        out_shape=(
            jax.ShapeDtypeStruct((27, 64, 64), F32),
            jax.ShapeDtypeStruct((512, 128), F32),
            jax.ShapeDtypeStruct((128, 256), F32),
        ),
        in_specs=[vmem],
        out_specs=(vmem,) * 3,
        scratch_shapes=[
            pltpu.VMEM((np_, 64, 128), BF),
            pltpu.VMEM((np_, 64, 128), BF),
            pltpu.VMEM((np_, 64, 128), BF),
            pltpu.VMEM((np_, 64, 128), BF),
            pltpu.VMEM((64, 128), BF),
            pltpu.VMEM((nz, 64, 128), BF),
            pltpu.VMEM((NC, np_, 64, 128), BF),
            dma((4,)), dma((4,)), dma((np_,)), dma((np_,)), dma((nz,)), dma((nz,)),
            dma((np_,)), dma((np_,)), dma((np_,)), dma((np_,)),
        ],
        compiler_params=pltpu.CompilerParams(collective_id=1, has_side_effects=True),
        name="reduce",
    )(part)


def tap_tables():
    ids = np.arange(8)
    target = np.zeros((9, 2, 2, 8, 4, 4), np.float32)
    choose = np.zeros((9, 2, 2, 4, 4, 9), np.float32)
    for a in range(3):
        for b in range(3):
            for x in range(8):
                for y in range(8):
                    xx, yy = x + a - 1, y + b - 1
                    dx, dy = (xx + 8) // 8, (yy + 8) // 8
                    choose[3 * a + b, x % 2, y % 2, x // 2, y // 2, 3 * dx + dy] = 1.0
                    for n in ids:
                        px, py = n // 4 + dx - 1, n % 4 + dy - 1
                        if py < 0 or py > 3:
                            spot = -1
                        elif px < 0:
                            spot = 512 + py * 8 + yy % 8
                        elif px > 1:
                            spot = 544 + py * 8 + yy % 8
                        else:
                            spot = (px * 4 + py) * 64 + xx % 8 * 8 + yy % 8
                        target[3 * a + b, x % 2, y % 2, n, x // 2, y // 2] = spot
    return target, choose


def shards(features, occupancy, neighbours, owners, w_conv, w_down, w_point, cotangent):
    nz = lax.axis_size("brick") // (NX * NC)
    ny = lax.axis_size("dp")
    flat = jnp.pad(features[0].reshape(8, 8, 8, 512), ((0, 0), (0, 0), (0, 0), (64, 64)))
    up_face = flat[4:8, 7].reshape(32, 640)
    down_face = flat[0:4, 0].reshape(32, 640)
    source = flat.reshape(512, 640)

    target, choose = tap_tables()
    linked = (neighbours[0].reshape(8, 9, 3)[:, :, 1] >= 0).astype(F32)
    flags = jnp.sum(choose[:, :, :, None] * linked[None, None, None, :, None, None, :], axis=-1)
    tgt = jnp.where(flags > 0, target, -1.0)
    tgt = jnp.pad(tgt.reshape(9, 512).T, ((0, 0), (0, 7)))
    occ = occupancy[0].reshape(8, 4, 2, 4, 2, 8).transpose(2, 4, 0, 1, 3, 5).reshape(512, 8).astype(BF)
    w9 = w_conv.reshape(9, 192, 64)
    u = jnp.concatenate(
        [jnp.pad(w9, ((0, 0), (0, 64), (0, 0))), jnp.pad(w9, ((0, 0), (64, 0), (0, 0)))], axis=2
    )
    slot_dev = owners[0] // 8
    dec = jnp.stack([slot_dev % NC, slot_dev // (NX * NC), owners[0] % 8, slot_dev // NC % NX])
    dec = jnp.pad(dec, ((0, 4), (0, 120)))
    before, after, cot = exchange(nz, up_face, down_face, cotangent[0], dec)
    part = compute(
        source, before, after, tgt, occ, u, w_down.reshape(512, 128), w_point, cot.reshape(512, 256)
    )
    gwc, gwd, gwp = reduce_all(nz, ny, part)
    return gwc.reshape(3, 3, 3, 64, 64), gwd.reshape(2, 2, 2, 64, 128), gwp


def solution(mesh):
    in_specs = (
        P("dp", "brick", None, None),
        P("dp", "brick", None),
        P("dp", "brick", None),
        P("dp", "brick"),
        P(),
        P(),
        P(),
        P("dp", "brick", None, None),
    )
    return jax.shard_map(shards, mesh=mesh, in_specs=in_specs, out_specs=(P(), P(), P()), check_vma=False)
```

time: 523 us -> 111 us (0.21); the launches traced: 517 us -> 111 us
  waiting for transfers between devices: 299 us -> 0 us
  Pallas kernels: 0 us -> 95.7 us
  local copies, waits for them, and re-layouts: 104 us -> 10.2 us
  starting transfers between devices: 36 us -> 0 us
  other arithmetic: 35.2 us -> 4.49 us
  matrix products: 26.6 us -> 0 us
  between operations: 15.2 us -> 0.76 us
    psum x1 -> x0, waiting for transfers between devices: 258 us -> none  [shards(): summed = lax.psum((grad_w_conv, grad_w_down, grad_w_point), ('dp', 'brick'))]
    pallas_call x0 -> x3, Pallas kernels: none -> 95.7 us  [the longest x1 49.8 us: exchange(): pl.pallas_call(lambda *refs: exchange_kernel(nz, *refs), out_shape=(jax.S...]
    gather x50 -> x0, local copies, waits for them, and re-layouts: 48.1 us -> none  [the longest x48 46 us: assemble(): jnp.take(window_part, indices[a][:, 9 * a + 3 * b + c], axis=0, mode='clip')]
    all_to_all x3 -> x0, waiting for transfers between devices: 41.4 us -> none  [the longest x1 28.1 us: shards(): lax.all_to_all(send_rows, 'brick', split_axis=0, concat_axis=0, tiled=True)]
    all_to_all x3 -> x0, starting transfers between devices: 29.5 us -> none  [the longest x1 12.9 us: shards(): lax.all_to_all(slot_out, 'brick', split_axis=0, concat_axis=0, tiled=True)]
    unnamed x117 -> x16, local copies, waits for them, and re-layouts: 26.5 us -> 4.93 us
    dot_general x33 -> x0, matrix products: 19.9 us -> none  [the longest x27 14.9 us: shards(): lax.dot_general(window_part, flat_grad, (((0,), (0,)), ((), ())), preferr...]
    slice x27 -> x1, local copies, waits for them, and re-layouts: 17.3 us -> 0.01 us  [shards(): linked = (neighbours[0].reshape(8, 9, 3)[:, :, 1] >= 0).astype(F32)]
  transfers between devices with their start and end apart: 6 -> 0, of which waited for: 3 -> 0; matrix products, arithmetic and copies ran while one was open for 6% -> 0% of each run, Pallas kernels for 0% -> 0%
where the time goes in v1:
time: 111 us
  Pallas kernels  95.7 us (86%)
  local copies, waits for them, and re-layouts  10.2 us (9%)
  other arithmetic  4.49 us (4%)
    pallas_call x1, Pallas kernels, exchange(): pl.pallas_call(lambda *refs: exchange_kernel(nz, *refs), out_shape=(jax.S...  49.8 us
    pallas_call x1, Pallas kernels, reduce_all(): pl.pallas_call(lambda *refs: reduce_kernel(nz, ny, *refs), out_shape=(jax...  30.4 us
    pallas_call x1, Pallas kernels, compute(): pl.pallas_call(compute_kernel, out_shape=jax.ShapeDtypeStruct((32, 64, 12...  15.5 us
    unnamed x16, local copies, waits for them, and re-layouts  4.93 us

profile of v1, /device:TPU:1, one launch (start us, length us, event | category | flops | bytes accessed | tf_op | source)
XLA Modules:
  0.0 111.1 jit_solution(1892513931245802980)
XLA Ops:
  0.6 0.0 copy-start.2
  0.6 0.7 and_select_fusion.4
  1.4 0.6 pad.21.refs_3_
  2.0 0.7 convert_element_type.29
  2.7 0.8 copy.24
  3.5 0.1 copy.28
  3.6 0.2 convert_element_type.30
  3.8 0.7 copy.27
  4.5 1.7 %multiply_reduce_fusion = f32[9,2,2,8,4,4]{3,5,4,2,1,0:T(4,128)S(1)} fusion(f32[8,9]{1,0:T(8,128)S(1)} %convert_bitcast_fusion, f32[9,2,2,4,4,9]{5,4,3,2,1,0:T(4,128)} %constant.94), kind=kLoop, calls=%fused_computation | loop fusion | flops 78336 | bytes 39456 | tf_op jit(solution)/shard_map/reduce_sum | solution.py:444
  6.2 0.0 copy-done.2
  6.2 0.0 copy-start.1
  6.2 0.1 compare_select_fusion
  6.4 0.0 copy-start
  6.4 0.5 copy.26
  6.9 0.7 pad.22.tgt_ref
  7.6 0.0 copy-done.1
  7.6 1.2 %fusion.2.u_ref = bf16[9,256,128]{2,1,0:T(8,128)(2,1)} fusion(bf16[9,192,64]{2,1,0:T(8,128)(2,1)S(1)} %bitcast.27), kind=kLoop, calls=%fused_computation.5 | loop fusion | flops 2359296 | bytes 811008 | tf_op jit(solution)/shard_map/concatenate | solution.py:449
  8.8 0.0 copy-done
  8.8 0.5 copy.23
  9.2 0.6 reshape_squeeze.13
  9.9 0.7 slice_bitcast_fusion
  10.6 1.2 %pad.20 = bf16[8,8,8,640]{3,2,1,0:T(8,128)(2,1)} pad(bf16[8,8,8,512]{3,2,1,0:T(8,128)(2,1)S(1)} %reshape_squeeze.13, bf16[]{:T(256)} %constant.66.clone.1), padding=0_0x0_0x0_0x64_64 | pad | bytes 1179650 | tf_op jit(solution)/shard_map/jit(_pad)/pad | solution.py:437
  11.8 49.8 %exchange.1 = (bf16[32,640]{1,0:T(8,128)(2,1)}, bf16[32,640]{1,0:T(8,128)(2,1)}, bf16[8,64,256]{2,1,0:T(8,128)(2,1)}) custom-call(bf16[32,640]{1,0:T(8,128)(2,1)} %get-tuple-element.18.refs_0_, bf16[32,640]{1,0:T(8,128)(2,1)} %get-tuple-element.17.refs_1_, bf16[8,64,256]{2,1,0:T(8,128)(2,1)} %bitcast.29, s32[8,128]{1,0:T(8,128)} %pad.21.refs_3_), custom_call_target="tpu_custom_call" | custom-call | tf_op jit(solution)/shard_map/exchange/pallas_call | solution.py:153
  61.6 15.5 %compute.1.refs_0_ = f32[32,64,128]{2,1,0:T(8,128)} custom-call(bf16[512,640]{1,0:T(8,128)(2,1)} %bitcast.23, bf16[32,640]{1,0:T(8,128)(2,1)} %get-tuple-element.9.before_ref, bf16[32,640]{1,0:T(8,128)(2,1)} %get-tuple-element.10.after_ref, f32[512,16]{1,0:T(8,128)} %pad.22.tgt_ref, bf16[512,8]{1,0:T(8,128)(2,1)} %bitcast.26, ...), custom_call_target="tpu_custom_call" | custom-call | tf_op jit(solution)/shard_map/compute/pallas_call | solution.py:281
  77.1 30.4 %reduce.1 = (f32[27,64,64]{2,1,0:T(8,128)}, f32[512,128]{1,0:T(8,128)}, f32[128,256]{1,0:T(8,128)}) custom-call(f32[32,64,128]{2,1,0:T(8,128)} %compute.1.refs_0_), custom_call_target="tpu_custom_call" | custom-call | tf_op jit(solution)/shard_map/reduce/pallas_call | solution.py:384
  107.5 0.0 copy-start.3
  107.5 0.0 copy-start.4
  107.5 2.2 %copy.32 = f32[3,3,3,64,64]{4,3,2,1,0:T(8,128)} copy(f32[3,3,3,64,64]{4,3,2,1,0:T(8,128)} %bitcast.25) | data formatting | bytes 884736
  109.7 0.0 copy-done.3
  109.7 0.7 copy.33
  110.4 0.0 copy-done.4
  110.4 0.7 copy.34
  (5 shorter events, 0.1 us)
Async XLA Ops:
  0.6 5.6 %copy-start.2 = (f32[9,2,2,8,4,4]{3,5,4,2,1,0:T(4,128)S(1)}, f32[9,2,2,8,4,4]{3,5,4,2,1,0:T(4,128)}, u32[]{:S(2)}) copy-start(f32[9,2,2,8,4,4]{3,5,4,2,1,0:T(4,128)} %constant.78.clone) | copy-start | bytes 55300
  6.2 1.4 %copy-start.1 = (bf16[3,3,3,64,64]{4,3,2,1,0:T(8,128)(2,1)S(1)}, bf16[3,3,3,64,64]{4,3,2,1,0:T(8,128)(2,1)}, u32[]{:S(2)}) copy-start(bf16[3,3,3,64,64]{4,3,2,1,0:T(8,128)(2,1)} %param.14) | copy-start | bytes 663556
  6.4 2.4 %copy-start = (bf16[1,8,512,64]{2,3,1,0:T(8,128)(2,1)S(1)}, bf16[1,8,512,64]{2,3,1,0:T(8,128)(2,1)}, u32[]{:S(2)}) copy-start(bf16[1,8,512,64]{2,3,1,0:T(8,128)(2,1)} %param.10) | copy-start | bytes 1572868
  107.5 2.2 %copy-start.3 = (f32[512,128]{1,0:T(8,128)S(1)}, f32[512,128]{1,0:T(8,128)}, u32[]{:S(2)}) copy-start(f32[512,128]{1,0:T(8,128)} %get-tuple-element.13) | copy-start | bytes 786436
  107.5 2.9 %copy-start.4 = (f32[128,256]{1,0:T(8,128)S(1)}, f32[128,256]{1,0:T(8,128)}, u32[]{:S(2)}) copy-start(f32[128,256]{1,0:T(8,128)} %get-tuple-element.27) | copy-start | bytes 393220

commit v2 on v0

v2 whole, which is shorter than its diff:
```python
import jax
import jax.numpy as jnp
import numpy as np
from jax import lax
from jax.experimental import pallas as pl
from jax.experimental.pallas import tpu as pltpu
from jax.sharding import PartitionSpec as P

MESH = pl.DeviceIdType.MESH
NX = 4
NC = 2
NSUB = 4
NB = 8
BF = jnp.bfloat16
F32 = jnp.float32


def where_am_i():
    spot = lax.axis_index("brick")
    return spot // (NX * NC), spot // NC % NX, spot % NC


def brick_at(z, x, c):
    return (z * NX + x) * NC + c


def greet(mates):
    barrier = pltpu.get_barrier_semaphore()
    for mate in mates:
        pl.semaphore_signal(barrier, inc=1, device_id=mate, device_id_type=MESH)
    pl.semaphore_wait(barrier, len(mates))


def slope_of(v):
    g = 1.0 / (1.0 + jnp.exp(-v))
    return g * (1.0 + v * (1.0 - g))


def silu_of(v):
    return v / (1.0 + jnp.exp(-v))


def dot(a, b, ca=1, cb=0):
    return lax.dot_general(a, b, (((ca,), (cb,)), ((), ())), preferred_element_type=F32)


RIGHT = ((1, 0), (1, 1), (1, 2), (2, 0), (2, 1), (2, 2), (1, 3), (3, 0), (3, 1), (3, 2), (2, 3), (4, 0), (4, 2), (3, 3))
LEFT = ((1, 1), (1, 0), (1, 3), (2, 1), (2, 0), (2, 3), (1, 2), (3, 1), (3, 0), (3, 3), (2, 2), (4, 1), (4, 3), (3, 2))
LAG = 3


def iota(shape, dim):
    return lax.broadcasted_iota(jnp.int32, shape, dim)


def ones_where(mask):
    return jnp.where(mask, 1.0, 0.0).astype(BF)


def tap_targets(near):
    row, tap = iota((512, 16), 0), iota((512, 16), 1)
    n = row // 16 % 8
    x = row // 4 % 4 * 2 + row // 256 + tap // 3 - 1
    y = row % 4 * 2 + row // 128 % 2 + tap % 3 - 1
    dx, dy = (x + 8) // 8, (y + 8) // 8
    px, py = n // 4 + dx - 1, n % 4 + dy - 1
    yy = (y + 8) % 8
    inner = (x + 8) % 8 * 64 + (px * 4 + py) * 8 + yy
    spot = jnp.where(px < 0, 512 + py * 8 + yy, jnp.where(px > 1, 544 + py * 8 + yy, inner))
    linked = ones_where(near >= 0)
    narrow = ones_where(iota((27, 16), 0) == 3 * iota((27, 16), 1) + 1)
    linked = dot(linked, narrow).astype(BF)
    brick = ones_where(iota((512, 8), 0) // 16 % 8 == iota((512, 8), 1))
    by_row = dot(brick, linked)
    code = 3 * dx + dy
    flag = jnp.zeros((512, 16), F32)
    for d in range(9):
        flag = flag + jnp.where(code == d, by_row[:, d : d + 1], 0.0)
    return jnp.where(flag > 0.5, spot.astype(F32), -1.0)


def occupied_at(occ):
    row, lane = iota((512, 512), 0), iota((512, 512), 1)
    brick = ones_where(iota((512, 8), 0) // 16 % 8 == iota((512, 8), 1))
    every = dot(brick, occ.astype(F32).astype(BF))
    mine = (row // 4 % 4 * 2 + row // 256) * 8 + row % 4 * 2 + row // 128 % 2
    own = jnp.where(lane // 8 == mine, every, 0.0).astype(BF)
    spread = ones_where(row % 8 == lane // 64)
    return dot(own, spread)


def step_kernel(
    nz, ny, src_ref, cot_ref, own_v, own_s, near_ref, occ_ref, w_ref, wd_ref, wp_ref,
    gwc_ref, gwd_ref, gwp_ref,
    source, halo_in, pool0, pool1, pool2, pool3, picked, landed, dec_in, dec_s,
    taps, pre, occ_at, hid_t, gpre_t, sums, part, cot_here,
    tosend, arrived, plane_out, plane_in, depth_out, depth_in, full,
    halo_send, halo_recv, dec_send, dec_recv, dec_sem,
    right_send, right_recv, left_send, left_recv, mate_send, mate_recv, row_send, row_recv,
    pair_send, pair_recv, plane_send, plane_recv, depth_send, depth_recv,
    back_send, back_recv, share_send, share_recv,
):
    z, x, c = where_am_i()
    y = lax.axis_index("dp")
    spot = lax.axis_index("brick")
    many = nz * NX * NC
    np_ = ny * NX
    me = y * NX + x

    def at(yy, brick):
        return {"dp": yy, "brick": brick}

    right, left = at(y, brick_at((z + 1) % nz, x, c)), at(y, brick_at((z + nz - 1) % nz, x, c))
    pair = at(y, brick_at(z, x, 1 - c))
    row = [at(y, brick_at(z, (x + g) % NX, c)) for g in range(1, NX)]
    ahead, behind = at(y, (spot + 1) % many), at(y, (spot + many - 1) % many)
    plane = []
    for g in range(1, np_):
        yy, xx = (y + g // NX) % ny, (x + g % NX) % NX
        plane.append((at(yy, brick_at(z, xx, c)), yy * NX + xx, g))
    depth = [at(y, brick_at((z + g) % nz, x, c)) for g in range(1, nz)]
    greet([pair, ahead, behind] + [p[0] for p in plane] + depth)

    pools = [pool0, pool1, pool2, pool3]
    pending = []

    def send(src, dst, ssem, rsem, mate):
        copy = pltpu.make_async_remote_copy(
            src_ref=src, dst_ref=dst, send_sem=ssem, recv_sem=rsem, device_id=mate, device_id_type=MESH
        )
        copy.start()
        pending.append(copy)
        return copy

    rows_src = src_ref.shape[0]
    halo_up = send(src_ref.at[pl.ds(rows_src - 32, 32)], halo_in.at[0], halo_send.at[0], halo_recv.at[0], ahead)
    halo_down = send(src_ref.at[pl.ds(0, 32)], halo_in.at[1], halo_send.at[1], halo_recv.at[1], behind)
    dec_copies = [send(own_v, dec_in.at[g], dec_send.at[g], dec_recv.at[g], row[g]) for g in range(NX - 1)]
    cells = cot_ref.shape[1] // NSUB
    rights, lefts, mates, rows = {}, {}, {}, {}

    def own(k):
        return cot_ref.at[:, pl.ds(k * cells, cells), :]

    def go_right(s, k):
        if s == 1:
            rights[1, k] = send(own(k), pools[k].at[c, z], right_send.at[0, k], right_recv.at[0, k], right)
            return
        rights[s - 1, k].wait_recv()
        home = pools[k].at[c, (z + nz - s + 1) % nz]
        rights[s, k] = send(home, home, right_send.at[s - 1, k], right_recv.at[s - 1, k], right)
        mates[s - 1, k] = send(home, home, mate_send.at[s - 1, k], mate_recv.at[s - 1, k], pair)

    def go_left(s, k):
        if s == 1:
            lefts[1, k] = send(own(k), pools[k].at[c, z], left_send.at[0, k], left_recv.at[0, k], left)
            return
        lefts[s - 1, k].wait_recv()
        home = pools[k].at[c, (z + s - 1) % nz]
        lefts[s, k] = send(home, home, left_send.at[s - 1, k], left_recv.at[s - 1, k], left)
        t = nz - s + 1
        mates[t, k] = send(home, home, mate_send.at[t, k], mate_recv.at[t, k], pair)

    def end_right(s, k):
        rights[s, k].wait_recv()
        home = pools[k].at[c, (z + nz - s) % nz]
        mates[s, k] = send(home, home, mate_send.at[s, k], mate_recv.at[s, k], pair)

    def end_left(s, k):
        lefts[s, k].wait_recv()
        home = pools[k].at[c, (z + s) % nz]
        t = nz - s
        mates[t, k] = send(home, home, mate_send.at[t, k], mate_recv.at[t, k], pair)

    def pick(g, k, b):
        o = dec_s[g, 0, b]
        return pools[k][o // NB % NC, o // (NB * NC * NX), o % NB]

    def start_rows(k):
        for t in range(nz):
            mates[t, k].wait_recv()
        for g in range(NX - 1):
            for b in range(NB):
                picked[g, k, b] = pick(NX - 2 - g, k, b)
            rows[g, k] = send(picked.at[g, k], landed.at[x, k], row_send.at[g, k], row_recv.at[g, k], row[g])
        for b in range(NB):
            landed[x, k, b] = pick(NX - 1, k, b)

    hold = {}

    def ready():
        for k in range(NSUB):
            mates[0, k] = send(own(k), pools[k].at[c, z], mate_send.at[0, k], mate_recv.at[0, k], pair)
            pools[k][c, z] = cot_ref[:, k * cells : (k + 1) * cells, :]
        source[0:512] = src_ref[...]
        hold["tgt"] = tap_targets(near_ref[...])
        occ_at[...] = occupied_at(occ_ref[...])

    def asks():
        for g in range(NX - 1):
            dec_copies[g].wait_recv()
        local = [pltpu.make_async_copy(dec_in.at[g], dec_s.at[g], dec_sem.at[g]) for g in range(NX - 1)]
        local.append(pltpu.make_async_copy(own_v, dec_s.at[NX - 1], dec_sem.at[NX - 1]))
        for copy in local:
            copy.start()
        for copy in local:
            copy.wait()

    def halo():
        halo_up.wait_recv()
        halo_down.wait_recv()
        source[512:544] = halo_in[0]
        source[544:576] = halo_in[1]

    def tap_step(tap):
        spots = iota((512, 576), 1).astype(F32)
        take = jnp.where(spots == hold["tgt"][:, tap : tap + 1], 1.0, 0.0).astype(BF)
        moved = dot(take, source[...]).astype(BF)
        taps[tap] = moved
        w = w_ref[tap]
        low = dot(w, ones_where(iota((64, 128), 0) == iota((64, 128), 1)))
        high = dot(w, ones_where(iota((64, 128), 0) + 64 == iota((64, 128), 1)))
        blank = jnp.zeros((64, 128), F32)
        u = (jnp.concatenate([low, blank], axis=0) + jnp.concatenate([blank, high], axis=0)).astype(BF)
        for t in range(4):
            lanes = slice(128 * t, 128 * t + 128)
            got = dot(moved[:, 128 * t : 128 * t + 256], u)
            pre[:, lanes] = got if tap == 0 else pre[:, lanes] + got

    def hide(ij):
        a = slice(128 * ij, 128 * ij + 128)
        hidden = (silu_of(pre[a, :]) * occ_at[a, :]).astype(BF)
        for r in range(4):
            hid_t[128 * r : 128 * r + 128, a] = hidden[:, 128 * r : 128 * r + 128]

    def coarsen():
        down = dot(hid_t[...], wd_ref[...])
        coarse = silu_of(down).astype(BF)
        hold["slope"] = slope_of(down)
        hold["coarse"] = coarse
        hold["point"] = slope_of(dot(coarse, wp_ref[...]))

    def reslope(ij):
        a = slice(128 * ij, 128 * ij + 128)
        pre[a, :] = occ_at[a, :] * slope_of(pre[a, :])

    jobs = [asks, halo]
    jobs += [lambda tap=tap: tap_step(tap) for tap in range(9)]
    jobs += [lambda ij=ij: hide(ij) for ij in range(4)]
    jobs += [coarsen]
    jobs += [lambda ij=ij: reslope(ij) for ij in range(4)]

    def work():
        if jobs:
            jobs.pop(0)()

    ends = {}
    for i, (s, k) in enumerate(RIGHT):
        if (s + 1, k) not in RIGHT:
            ends.setdefault(i + LAG, []).append((end_right, s, k))
    for i, (s, k) in enumerate(LEFT):
        if (s + 1, k) not in LEFT:
            ends.setdefault(i + LAG, []).append((end_left, s, k))
    left_over = {k: 0 for k in range(NSUB)}
    for group in ends.values():
        for _, s, k in group:
            left_over[k] += 1
    done, started = dict(left_over), []
    waiting = []
    for i in range(len(RIGHT) + LAG):
        if i < len(RIGHT):
            go_right(*RIGHT[i])
            go_left(*LEFT[i])
        for f, s, k in ends.get(i, []):
            f(s, k)
            done[k] -= 1
            if done[k] == 0:
                waiting.append((i, k))
        if i == 2:
            ready()
        if i >= 3:
            work()
            work()
        while waiting and waiting[0][0] < i:
            start_rows(waiting.pop(0)[1])
    while waiting:
        start_rows(waiting.pop(0)[1])
    while jobs:
        work()

    order_row, order_col = iota((512, 512), 0), iota((512, 512), 1)
    order = ones_where(order_col == 4 * (order_row % 128) + order_row // 128)
    for k in range(NSUB):
        for g in range(NX - 1):
            rows[g, k].wait_recv()
    for b in range(NB):
        o = dec_s[NX - 1, 0, b]
        for k in range(NSUB):
            lo = b * NSUB * cells + k * cells
            cot_here[lo : lo + cells, :] = landed[o // (NB * NC) % NX, k, b]

    cot = dot(order, cot_here[...])
    gpoint = (cot * hold["point"]).astype(BF)
    gwp = dot(hold["coarse"], gpoint, 0, 0)
    gplaced = dot(gpoint, wp_ref[...], 1, 1).astype(BF)
    gdown = (gplaced.astype(F32) * hold["slope"]).astype(BF)
    gwd = dot(hid_t[...], gdown, 0, 0)
    ghid = dot(gdown, wd_ref[...], 1, 1)
    for r in range(4):
        for ij in range(4):
            a = slice(128 * ij, 128 * ij + 128)
            b = slice(128 * r, 128 * r + 128)
            gpre_t[b, a] = (ghid[b, a] * pre[a, b]).astype(BF).T
    for j in range(8):
        part[14 + j] = gwd[64 * j : 64 * j + 64, :]
    for j in range(4):
        r, t = j % 2, j // 2
        part[22 + j] = gwp[64 * r : 64 * r + 64, 128 * t : 128 * t + 128]
    for tap in range(9):
        total = jnp.zeros((128, 256), F32)
        for t in range(4):
            total += dot(gpre_t[128 * t : 128 * t + 128, :], taps[tap, :, 128 * t : 128 * t + 256])
        sums[tap] = total.T
    low = iota((64, 128), 1) < 64

    def block(m):
        tap, c3 = m // 3, m % 3
        return sums[tap, 64 * c3 : 64 * c3 + 64, :], sums[tap, 64 * c3 + 64 : 64 * c3 + 128, :]

    for j in range(14):
        a0, a1 = block(2 * j)
        even = a0 + pltpu.roll(a1, 64, 1)
        if 2 * j + 1 < 27:
            b0, b1 = block(2 * j + 1)
            odd = pltpu.roll(b0, 64, 1) + b1
        else:
            odd = jnp.zeros_like(even)
        part[j] = jnp.where(low, even, odd)
    for j in range(26, 32):
        part[j] = jnp.zeros((64, 128), F32)

    pieces = 4
    size = np_ // pieces
    firsts = []
    for i in range(pieces):
        tosend[pl.ds(i * size, size)] = part[pl.ds((1 - c) * np_ + i * size, size)].astype(BF)
        at = pl.ds(i * size, size)
        firsts.append(send(tosend.at[at], arrived.at[at], pair_send.at[i], pair_recv.at[i], pair))
    for i in range(pieces):
        firsts[i].wait_recv()
        at = pl.ds(i * size, size)
        plane_out[at] = (part[pl.ds(c * np_ + i * size, size)] + arrived[at].astype(F32)).astype(BF)
    seconds = [
        send(plane_out.at[k], plane_in.at[g], plane_send.at[g], plane_recv.at[g], mate) for mate, k, g in plane
    ]
    total = plane_out[me].astype(F32)
    for g in range(1, np_):
        seconds[g - 1].wait_recv()
        total += plane_in[g].astype(F32)
    depth_out[...] = total.astype(BF)
    thirds = [
        send(depth_out, depth_in.at[z], depth_send.at[g], depth_recv.at[g], mate) for g, mate in enumerate(depth)
    ]
    depth_in[z] = total.astype(BF)
    for copy in thirds:
        copy.wait_recv()
    total = depth_in[0].astype(F32)
    for k in range(1, nz):
        total += depth_in[k].astype(F32)
    mine = full.at[c, me]
    full[c, me] = total.astype(BF)
    backs = [send(mine, mine, back_send.at[g], back_recv.at[g], mate) for mate, k, g in plane]
    shares = [send(mine, mine, share_send.at[0], share_recv.at[0], pair)]
    for g in range(1, np_):
        backs[g - 1].wait_recv()
        yy, xx = (y + ny - g // NX) % ny, (x + NX - g % NX) % NX
        home = full.at[c, yy * NX + xx]
        shares.append(send(home, home, share_send.at[g], share_recv.at[g], pair))
    for copy in shares:
        copy.wait_recv()
    for j in range(14):
        chunk = full[j // np_, j % np_].astype(F32)
        gwc_ref[2 * j] = chunk[:, :64]
        if 2 * j + 1 < 27:
            gwc_ref[2 * j + 1] = pltpu.roll(chunk, 64, 1)[:, :64]
    for j in range(8):
        k = 14 + j
        gwd_ref[64 * j : 64 * j + 64, :] = full[k // np_, k % np_].astype(F32)
    for j in range(4):
        r, t = j % 2, j // 2
        k = 22 + j
        gwp_ref[64 * r : 64 * r + 64, 128 * t : 128 * t + 128] = full[k // np_, k % np_].astype(F32)
    for copy in pending:
        copy.wait_send()


def step(nz, ny, src, cot, owners, near, occ, w, wd, wp):
    slots, cells, wide = cot.shape
    chunk = (slots, cells // NSUB, wide)
    dma = pltpu.SemaphoreType.DMA
    vmem = pl.BlockSpec(memory_space=pltpu.VMEM)
    smem = pl.BlockSpec(memory_space=pltpu.SMEM)
    far = nz // 2
    np_ = ny * NX
    return pl.pallas_call(
        lambda *refs: step_kernel(nz, ny, *refs),
        out_shape=(
            jax.ShapeDtypeStruct((27, 64, 64), F32),
            jax.ShapeDtypeStruct((512, 128), F32),
            jax.ShapeDtypeStruct((128, 256), F32),
        ),
        in_specs=[vmem, vmem, vmem, smem] + [vmem] * 5,
        out_specs=(vmem,) * 3,
        scratch_shapes=[
            pltpu.VMEM((576, 640), BF),
            pltpu.VMEM((2, 32, 640), BF),
            *[pltpu.VMEM((NC, nz) + chunk, BF)] * NSUB,
            pltpu.VMEM((NX - 1, NSUB) + chunk, BF),
            pltpu.VMEM((NX, NSUB) + chunk, BF),
            pltpu.VMEM((NX - 1,) + owners.shape, jnp.int32),
            pltpu.SMEM((NX,) + owners.shape, jnp.int32),
            pltpu.VMEM((9, 512, 640), BF),
            pltpu.VMEM((512, 512), F32),
            pltpu.VMEM((512, 512), F32),
            pltpu.VMEM((512, 512), BF),
            pltpu.VMEM((512, 512), BF),
            pltpu.VMEM((9, 256, 128), F32),
            pltpu.VMEM((2 * np_, 64, 128), F32),
            pltpu.VMEM((slots * cells, wide), BF),
            pltpu.VMEM((np_, 64, 128), BF),
            pltpu.VMEM((np_, 64, 128), BF),
            pltpu.VMEM((np_, 64, 128), BF),
            pltpu.VMEM((np_, 64, 128), BF),
            pltpu.VMEM((64, 128), BF),
            pltpu.VMEM((nz, 64, 128), BF),
            pltpu.VMEM((NC, np_, 64, 128), BF),
            dma((2,)), dma((2,)), dma((NX - 1,)), dma((NX - 1,)), dma((NX,)),
            dma((far, NSUB)), dma((far, NSUB)), dma((far, NSUB)), dma((far, NSUB)),
            dma((nz, NSUB)), dma((nz, NSUB)), dma((NX - 1, NSUB)), dma((NX - 1, NSUB)),
            dma((4,)), dma((4,)), dma((np_,)), dma((np_,)), dma((nz,)), dma((nz,)),
            dma((np_,)), dma((np_,)), dma((np_,)), dma((np_,)),
        ],
        compiler_params=pltpu.CompilerParams(collective_id=0, has_side_effects=True),
        name="step",
    )(src, cot, owners, owners, near, occ, w, wd, wp)


def shards(features, occupancy, neighbours, owners, w_conv, w_down, w_point, cotangent):
    nz = lax.axis_size("brick") // (NX * NC)
    ny = lax.axis_size("dp")
    flat = features[0].reshape(8, 8, 8, 512).transpose(1, 0, 2, 3).reshape(512, 512)
    source = jnp.pad(flat, ((0, 0), (64, 64)))
    gwc, gwd, gwp = step(
        nz, ny, source, cotangent[0], owners, neighbours[0], occupancy[0],
        w_conv.reshape(9, 192, 64), w_down.reshape(512, 128), w_point,
    )
    return gwc.reshape(3, 3, 3, 64, 64), gwd.reshape(2, 2, 2, 64, 128), gwp


def solution(mesh):
    in_specs = (
        P("dp", "brick", None, None),
        P("dp", "brick", None),
        P("dp", "brick", None),
        P("dp", "brick"),
        P(),
        P(),
        P(),
        P("dp", "brick", None, None),
    )
    return jax.shard_map(shards, mesh=mesh, in_specs=in_specs, out_specs=(P(), P(), P()), check_vma=False)
```

time: 523 us -> 85.4 us (0.16); the launches traced: 517 us -> 85.2 us
  waiting for transfers between devices: 299 us -> 0 us
  local copies, waits for them, and re-layouts: 104 us -> 7.24 us
  Pallas kernels: 0 us -> 77.3 us
  starting transfers between devices: 36 us -> 0 us
  other arithmetic: 35.2 us -> 0 us
  matrix products: 26.6 us -> 0 us
  between operations: 15.2 us -> 0.67 us
    psum x1 -> x0, waiting for transfers between devices: 258 us -> none  [shards(): summed = lax.psum((grad_w_conv, grad_w_down, grad_w_point), ('dp', 'brick'))]
    pallas_call x0 -> x1, Pallas kernels: none -> 77.3 us  [step(): pl.pallas_call(lambda *refs: step_kernel(nz, ny, *refs), out_shape=(jax.S...]
    gather x50 -> x0, local copies, waits for them, and re-layouts: 48.1 us -> none  [the longest x48 46 us: assemble(): jnp.take(window_part, indices[a][:, 9 * a + 3 * b + c], axis=0, mode='clip')]
    all_to_all x3 -> x0, waiting for transfers between devices: 41.4 us -> none  [the longest x1 28.1 us: shards(): lax.all_to_all(send_rows, 'brick', split_axis=0, concat_axis=0, tiled=True)]
    all_to_all x3 -> x0, starting transfers between devices: 29.5 us -> none  [the longest x1 12.9 us: shards(): lax.all_to_all(slot_out, 'brick', split_axis=0, concat_axis=0, tiled=True)]
    unnamed x117 -> x8, local copies, waits for them, and re-layouts: 26.5 us -> 5.39 us
    dot_general x33 -> x0, matrix products: 19.9 us -> none  [the longest x27 14.9 us: shards(): lax.dot_general(window_part, flat_grad, (((0,), (0,)), ((), ())), preferr...]
    slice x27 -> x0, local copies, waits for them, and re-layouts: 17.3 us -> none  [the longest x22 15.4 us: assemble(): pools[a][:, :, SPANS[b][0]:SPANS[b][1], SPANS[c][0]:SPANS[c][1], :]]
  transfers between devices with their start and end apart: 6 -> 0, of which waited for: 3 -> 0; matrix products, arithmetic and copies ran while one was open for 6% -> 0% of each run, Pallas kernels for 0% -> 0%
where the time goes in v2:
time: 85.4 us; the launch traced here: 85.2 us
  Pallas kernels  77.3 us (91%)
  local copies, waits for them, and re-layouts  7.24 us (8%)
    pallas_call x1, Pallas kernels, step(): pl.pallas_call(lambda *refs: step_kernel(nz, ny, *refs), out_shape=(jax.S...  77.3 us
    unnamed x8, local copies, waits for them, and re-layouts  5.39 us

profile of v2, /device:TPU:1, one launch (start us, length us, event | category | flops | bytes accessed | tf_op | source)
XLA Modules:
  0.0 85.2 jit_solution(4410438325283444763)
XLA Ops:
  0.6 1.5 %copy.11 = bf16[1,8,512,64]{3,2,1,0:T(8,128)(2,1)S(1)} copy(bf16[1,8,512,64]{2,3,1,0:T(8,128)(2,1)} %param.8) | data formatting | bytes 1048576 | tf_op args[0]
  2.2 0.6 reshape_squeeze.3
  2.8 1.2 %pad.4.refs_0_ = bf16[512,640]{1,0:T(8,128)(2,1)} pad(bf16[512,512]{1,0:T(8,128)(2,1)S(1)} %bitcast.12, bf16[]{:T(256)} %constant.2.clone.1), padding=0_0x64_64 | pad | bytes 1179650 | tf_op jit(solution)/shard_map/jit(_pad)/pad | solution.py:452
  4.0 77.3 %step.1 = (f32[27,64,64]{2,1,0:T(8,128)}, f32[512,128]{1,0:T(8,128)}, f32[128,256]{1,0:T(8,128)}) custom-call(bf16[512,640]{1,0:T(8,128)(2,1)} %pad.4.refs_0_, bf16[8,64,256]{2,1,0:T(8,128)(2,1)} %bitcast.16, s32[1,8]{1,0:T(1,128)} %refs_3_.1, s32[1,8]{1,0:T(1,128)} %refs_3_.1, s32[8,27]{1,0:T(8,128)} %bitcast.19, s32[8,512]{1,0:T(8,128)} %bitcast.18, ...), custom_call_target="tpu_custom_call" | custom-call | tf_op jit(solution)/shard_map/step/pallas_call | solution.py:405
  81.3 0.0 copy-start
  81.3 2.2 %copy.16 = f32[3,3,3,64,64]{4,3,2,1,0:T(8,128)} copy(f32[3,3,3,64,64]{4,3,2,1,0:T(8,128)} %bitcast.13) | data formatting | bytes 884736
  83.5 0.0 copy-done
  83.5 0.0 copy-start.1
  83.5 0.7 copy.17
  84.2 0.3 copy-done.1
  84.5 0.7 copy.18
  (1 shorter events, 0.0 us)
Async XLA Ops:
  81.3 2.2 %copy-start = (f32[512,128]{1,0:T(8,128)S(1)}, f32[512,128]{1,0:T(8,128)}, u32[]{:S(2)}) copy-start(f32[512,128]{1,0:T(8,128)} %get-tuple-element.7) | copy-start | bytes 786436
  83.5 1.0 %copy-start.1 = (f32[128,256]{1,0:T(8,128)S(1)}, f32[128,256]{1,0:T(8,128)}, u32[]{:S(2)}) copy-start(f32[128,256]{1,0:T(8,128)} %get-tuple-element.14) | copy-start | bytes 393220

commit v3 on v2

--- a/solution.py
+++ b/solution.py
@@ -24,13 +24,6 @@
     return (z * NX + x) * NC + c
 
 
-def greet(mates):
-    barrier = pltpu.get_barrier_semaphore()
-    for mate in mates:
-        pl.semaphore_signal(barrier, inc=1, device_id=mate, device_id_type=MESH)
-    pl.semaphore_wait(barrier, len(mates))
-
-
 def slope_of(v):
     g = 1.0 / (1.0 + jnp.exp(-v))
     return g * (1.0 + v * (1.0 - g))
@@ -44,8 +37,8 @@
     return lax.dot_general(a, b, (((ca,), (cb,)), ((), ())), preferred_element_type=F32)
 
 
-RIGHT = ((1, 0), (1, 1), (1, 2), (2, 0), (2, 1), (2, 2), (1, 3), (3, 0), (3, 1), (3, 2), (2, 3), (4, 0), (4, 2), (3, 3))
-LEFT = ((1, 1), (1, 0), (1, 3), (2, 1), (2, 0), (2, 3), (1, 2), (3, 1), (3, 0), (3, 3), (2, 2), (4, 1), (4, 3), (3, 2))
+RIGHT = ((1, 0), (1, 1), (1, 2), (2, 0), (2, 1), (2, 2), (3, 0), (3, 1), (1, 3), (4, 0), (3, 2), (2, 3), (4, 2), (3, 3))
+LEFT = tuple((s, k ^ 1) for s, k in RIGHT)
 LAG = 3
 
 
@@ -57,43 +50,44 @@
     return jnp.where(mask, 1.0, 0.0).astype(BF)
 
 
+def brick_rows():
+    return ones_where((iota((512, 8), 0) >> 4 & 7) == iota((512, 8), 1))
+
+
 def tap_targets(near):
-    row, tap = iota((512, 16), 0), iota((512, 16), 1)
-    n = row // 16 % 8
-    x = row // 4 % 4 * 2 + row // 256 + tap // 3 - 1
-    y = row % 4 * 2 + row // 128 % 2 + tap % 3 - 1
-    dx, dy = (x + 8) // 8, (y + 8) // 8
-    px, py = n // 4 + dx - 1, n % 4 + dy - 1
-    yy = (y + 8) % 8
-    inner = (x + 8) % 8 * 64 + (px * 4 + py) * 8 + yy
-    spot = jnp.where(px < 0, 512 + py * 8 + yy, jnp.where(px > 1, 544 + py * 8 + yy, inner))
+    row, tap = iota((512, 1), 0), iota((1, 16), 1)
+    n = row >> 4 & 7
+    third = (tap * 11) >> 5
+    x = ((row >> 2 & 3) * 2 + (row >> 8)) + (third - 1)
+    y = ((row & 3) * 2 + (row >> 7 & 1)) + (tap - 3 * third - 1)
+    dx, dy = (x + 8) >> 3, (y + 8) >> 3
+    px, py = (n >> 2) + dx - 1, (n & 3) + dy - 1
+    side = py * 8 + (y & 7)
+    spot = side + jnp.where(px < 0, 512, jnp.where(px > 1, 544, (x & 7) * 64 + px * 32))
     linked = ones_where(near >= 0)
     narrow = ones_where(iota((27, 16), 0) == 3 * iota((27, 16), 1) + 1)
-    linked = dot(linked, narrow).astype(BF)
-    brick = ones_where(iota((512, 8), 0) // 16 % 8 == iota((512, 8), 1))
-    by_row = dot(brick, linked)
+    by_row = dot(brick_rows(), dot(linked, narrow).astype(BF))
     code = 3 * dx + dy
     flag = jnp.zeros((512, 16), F32)
     for d in range(9):
-        flag = flag + jnp.where(code == d, by_row[:, d : d + 1], 0.0)
+        flag = jnp.where(code == d, by_row[:, d : d + 1], flag)
     return jnp.where(flag > 0.5, spot.astype(F32), -1.0)
 
 
 def occupied_at(occ):
-    row, lane = iota((512, 512), 0), iota((512, 512), 1)
-    brick = ones_where(iota((512, 8), 0) // 16 % 8 == iota((512, 8), 1))
-    every = dot(brick, occ.astype(F32).astype(BF))
-    mine = (row // 4 % 4 * 2 + row // 256) * 8 + row % 4 * 2 + row // 128 % 2
-    own = jnp.where(lane // 8 == mine, every, 0.0).astype(BF)
-    spread = ones_where(row % 8 == lane // 64)
+    row, lane = iota((512, 1), 0), iota((1, 512), 1)
+    every = dot(brick_rows(), occ.astype(F32).astype(BF))
+    mine = ((row >> 2 & 3) * 2 + (row >> 8)) * 8 + (row & 3) * 2 + (row >> 7 & 1)
+    own = jnp.where((lane >> 3) == mine, every, 0.0).astype(BF)
+    spread = ones_where((row & 7) == (lane >> 6))
     return dot(own, spread)
 
 
 def step_kernel(
     nz, ny, src_ref, cot_ref, own_v, own_s, near_ref, occ_ref, w_ref, wd_ref, wp_ref,
     gwc_ref, gwd_ref, gwp_ref,
-    source, halo_in, pool0, pool1, pool2, pool3, picked, landed, dec_in, dec_s,
-    taps, pre, occ_at, hid_t, gpre_t, sums, part, cot_here,
+    source, halo_in, pool0, pool1, pool2, pool3, picked, far_in, land0, land1, land2, land3, dec_in, dec_s,
+    taps, pre, occ_at, hid_t, gpre_t, sums, part, cot_here, order_at,
     tosend, arrived, plane_out, plane_in, depth_out, depth_in, full,
     halo_send, halo_recv, dec_send, dec_recv, dec_sem,
     right_send, right_recv, left_send, left_recv, mate_send, mate_recv, row_send, row_recv,
@@ -119,8 +113,17 @@
         yy, xx = (y + g // NX) % ny, (x + g % NX) % NX
         plane.append((at(yy, brick_at(z, xx, c)), yy * NX + xx, g))
     depth = [at(y, brick_at((z + g) % nz, x, c)) for g in range(1, nz)]
-    greet([pair, ahead, behind] + [p[0] for p in plane] + depth)
-
+    mates_all = [pair, ahead, behind] + [p[0] for p in plane] + depth
+    barrier = pltpu.get_barrier_semaphore()
+    for mate in mates_all:
+        pl.semaphore_signal(barrier, inc=1, device_id=mate, device_id_type=MESH)
+    for k in range(NSUB):
+        quarter = cot_ref.shape[1] // NSUB
+        (pool0, pool1, pool2, pool3)[k][c, z] = cot_ref[:, k * quarter : (k + 1) * quarter, :]
+    tgt = tap_targets(near_ref[...])
+    pl.semaphore_wait(barrier, len(mates_all))
+
+    lands = [land0, land1, land2, land3]
     pools = [pool0, pool1, pool2, pool3]
     pending = []
 
@@ -176,25 +179,46 @@
         o = dec_s[g, 0, b]
         return pools[k][o // NB % NC, o // (NB * NC * NX), o % NB]
 
+    fars, nears = {}, {}
+
     def start_rows(k):
         for t in range(nz):
             mates[t, k].wait_recv()
-        for g in range(NX - 1):
-            for b in range(NB):
-                picked[g, k, b] = pick(NX - 2 - g, k, b)
-            rows[g, k] = send(picked.at[g, k], landed.at[x, k], row_send.at[g, k], row_recv.at[g, k], row[g])
+        hop = 1 if k % 2 == 0 else NX - 1
         for b in range(NB):
-            landed[x, k, b] = pick(NX - 1, k, b)
+            picked[0, k, b] = pick(NX - 1 - NX // 2, k, b)
+        fars[k] = send(picked.at[0, k], far_in.at[k], row_send.at[0, k], row_recv.at[0, k], row[hop - 1])
+        back = NX - hop
+        for b in range(NB):
+            picked[1, k, b] = pick(NX - 1 - back, k, b)
+        nears[k] = send(picked.at[1, k], lands[k].at[2], row_send.at[1, k], row_recv.at[1, k], row[back - 1])
+        for b in range(NB):
+            lands[k][0, b] = pick(NX - 1, k, b)
+
+    def relay(k):
+        fars[k].wait_recv()
+        hop = 1 if k % 2 == 0 else NX - 1
+        g = NX - 1 - hop
+        for b in range(NB):
+            mine = dec_s[g, 0, b] // (NB * NC) % NX == x
+            picked[2, k, b] = jnp.where(mine, pick(g, k, b).astype(F32), far_in[k, b].astype(F32)).astype(BF)
+        rows[k] = send(picked.at[2, k], lands[k].at[1], row_send.at[2, k], row_recv.at[2, k], row[hop - 1])
+
+    def finish(k):
+        rows[k].wait_recv()
+        nears[k].wait_recv()
+        behind_x = (x + NX - 1) % NX if k % 2 == 1 else (x + 1) % NX
+        for b in range(NB):
+            source_x = dec_s[NX - 1, 0, b] // (NB * NC) % NX
+            which = jnp.where(source_x == x, 0, jnp.where(source_x == behind_x, 2, 1))
+            lo = b * NSUB * cells + k * cells
+            cot_here[lo : lo + cells, :] = lands[k][which, b]
 
     hold = {}
 
     def ready():
         for k in range(NSUB):
             mates[0, k] = send(own(k), pools[k].at[c, z], mate_send.at[0, k], mate_recv.at[0, k], pair)
-            pools[k][c, z] = cot_ref[:, k * cells : (k + 1) * cells, :]
-        source[0:512] = src_ref[...]
-        hold["tgt"] = tap_targets(near_ref[...])
-        occ_at[...] = occupied_at(occ_ref[...])
 
     def asks():
         for g in range(NX - 1):
@@ -209,12 +233,23 @@
     def halo():
         halo_up.wait_recv()
         halo_down.wait_recv()
-        source[512:544] = halo_in[0]
-        source[544:576] = halo_in[1]
+        low = iota((1, 128), 1) < 64
+
+        def shifted(lo, block):
+            size = block.shape[0]
+            last = jnp.zeros((size, 128), F32)
+            for t in range(5):
+                now = pltpu.roll(block[:, 128 * t : 128 * t + 128].astype(F32), 64, 1) if t < 4 else jnp.zeros((size, 128), F32)
+                source[lo : lo + size, 128 * t : 128 * t + 128] = jnp.where(low, last, now).astype(BF)
+                last = now
+
+        shifted(0, src_ref[...])
+        shifted(512, halo_in[0])
+        shifted(544, halo_in[1])
 
     def tap_step(tap):
-        spots = iota((512, 576), 1).astype(F32)
-        take = jnp.where(spots == hold["tgt"][:, tap : tap + 1], 1.0, 0.0).astype(BF)
+        spots = iota((1, 576), 1).astype(F32)
+        take = jnp.where(spots == tgt[:, tap : tap + 1], 1.0, 0.0).astype(BF)
         moved = dot(take, source[...]).astype(BF)
         taps[tap] = moved
         w = w_ref[tap]
@@ -244,11 +279,20 @@
         a = slice(128 * ij, 128 * ij + 128)
         pre[a, :] = occ_at[a, :] * slope_of(pre[a, :])
 
+    def occupy():
+        occ_at[...] = occupied_at(occ_ref[...])
+
+    def ordering():
+        r = iota((512, 1), 0)
+        order_at[...] = ones_where(iota((1, 512), 1) == 4 * (r & 127) + (r >> 7))
+
     jobs = [asks, halo]
     jobs += [lambda tap=tap: tap_step(tap) for tap in range(9)]
+    jobs += [occupy]
     jobs += [lambda ij=ij: hide(ij) for ij in range(4)]
     jobs += [coarsen]
     jobs += [lambda ij=ij: reslope(ij) for ij in range(4)]
+    jobs += [ordering]
 
     def work():
         if jobs:
@@ -265,8 +309,8 @@
     for group in ends.values():
         for _, s, k in group:
             left_over[k] += 1
-    done, started = dict(left_over), []
-    waiting = []
+    done = dict(left_over)
+    waiting, relays, finishes = [], [], []
     for i in range(len(RIGHT) + LAG):
         if i < len(RIGHT):
             go_right(*RIGHT[i])
@@ -282,24 +326,27 @@
             work()
             work()
         while waiting and waiting[0][0] < i:
-            start_rows(waiting.pop(0)[1])
+            k = waiting.pop(0)[1]
+            start_rows(k)
+            relays.append((i + LAG, k))
+        while relays and relays[0][0] <= i:
+            k = relays.pop(0)[1]
+            relay(k)
+            finishes.append(k)
     while waiting:
-        start_rows(waiting.pop(0)[1])
+        k = waiting.pop(0)[1]
+        start_rows(k)
+        relays.append((0, k))
+    for _, k in relays:
+        work()
+        relay(k)
+        finishes.append(k)
     while jobs:
         work()
-
-    order_row, order_col = iota((512, 512), 0), iota((512, 512), 1)
-    order = ones_where(order_col == 4 * (order_row % 128) + order_row // 128)
-    for k in range(NSUB):
-        for g in range(NX - 1):
-            rows[g, k].wait_recv()
-    for b in range(NB):
-        o = dec_s[NX - 1, 0, b]
-        for k in range(NSUB):
-            lo = b * NSUB * cells + k * cells
-            cot_here[lo : lo + cells, :] = landed[o // (NB * NC) % NX, k, b]
-
-    cot = dot(order, cot_here[...])
+    for k in finishes:
+        finish(k)
+
+    cot = dot(order_at[...], cot_here[...])
     gpoint = (cot * hold["point"]).astype(BF)
     gwp = dot(hold["coarse"], gpoint, 0, 0)
     gplaced = dot(gpoint, wp_ref[...], 1, 1).astype(BF)
@@ -413,10 +460,11 @@
         out_specs=(vmem,) * 3,
         scratch_shapes=[
             pltpu.VMEM((576, 640), BF),
-            pltpu.VMEM((2, 32, 640), BF),
+            pltpu.VMEM((2, 32, 512), BF),
             *[pltpu.VMEM((NC, nz) + chunk, BF)] * NSUB,
-            pltpu.VMEM((NX - 1, NSUB) + chunk, BF),
-            pltpu.VMEM((NX, NSUB) + chunk, BF),
+            pltpu.VMEM((3, NSUB) + chunk, BF),
+            pltpu.VMEM((NSUB,) + chunk, BF),
+            *[pltpu.VMEM((3,) + chunk, BF)] * NSUB,
             pltpu.VMEM((NX - 1,) + owners.shape, jnp.int32),
             pltpu.SMEM((NX,) + owners.shape, jnp.int32),
             pltpu.VMEM((9, 512, 640), BF),
@@ -427,6 +475,7 @@
             pltpu.VMEM((9, 256, 128), F32),
             pltpu.VMEM((2 * np_, 64, 128), F32),
             pltpu.VMEM((slots * cells, wide), BF),
+            pltpu.VMEM((512, 512), BF),
             pltpu.VMEM((np_, 64, 128), BF),
             pltpu.VMEM((np_, 64, 128), BF),
             pltpu.VMEM((np_, 64, 128), BF),
@@ -449,9 +498,8 @@
     nz = lax.axis_size("brick") // (NX * NC)
     ny = lax.axis_size("dp")
     flat = features[0].reshape(8, 8, 8, 512).transpose(1, 0, 2, 3).reshape(512, 512)
-    source = jnp.pad(flat, ((0, 0), (64, 64)))
     gwc, gwd, gwp = step(
-        nz, ny, source, cotangent[0], owners, neighbours[0], occupancy[0],
+        nz, ny, flat, cotangent[0], owners, neighbours[0], occupancy[0],
         w_conv.reshape(9, 192, 64), w_down.reshape(512, 128), w_point,
     )
     return gwc.reshape(3, 3, 3, 64, 64), gwd.reshape(2, 2, 2, 64, 128), gwp

time: 85.4 us -> 85.7 us (level)
    pad x1 -> x0, local copies, waits for them, and re-layouts: 1.2 us -> none  [shards(): source = jnp.pad(flat, ((0, 0), (64, 64)))]
where the time goes in v3:
time: 85.7 us; the launch traced here: 85.5 us
  Pallas kernels  78 us (91%)
  local copies, waits for them, and re-layouts  6.84 us (8%)
    pallas_call x1, Pallas kernels, step(): pl.pallas_call(lambda *refs: step_kernel(nz, ny, *refs), out_shape=(jax.S...  78 us
    unnamed x8, local copies, waits for them, and re-layouts  5.39 us

profile of v3, /device:TPU:1, one launch (start us, length us, event | category | flops | bytes accessed | tf_op | source)
XLA Modules:
  0.0 85.5 jit_solution(3144609910745107002)
XLA Ops:
  0.6 1.5 %copy.11 = bf16[1,8,512,64]{3,2,1,0:T(8,128)(2,1)S(1)} copy(bf16[1,8,512,64]{2,3,1,0:T(8,128)(2,1)} %param.8) | data formatting | bytes 1048576 | tf_op args[0]
  2.2 0.6 reshape_squeeze.3
  2.8 0.8 copy.12
  3.6 78.0 %step.1 = (f32[27,64,64]{2,1,0:T(8,128)}, f32[512,128]{1,0:T(8,128)}, f32[128,256]{1,0:T(8,128)}) custom-call(bf16[512,512]{1,0:T(8,128)(2,1)} %bitcast.12, bf16[8,64,256]{2,1,0:T(8,128)(2,1)} %bitcast.15, s32[1,8]{1,0:T(1,128)} %refs_3_.1, s32[1,8]{1,0:T(1,128)} %refs_3_.1, s32[8,27]{1,0:T(8,128)} %bitcast.19, s32[8,512]{1,0:T(8,128)} %bitcast.18, ...), custom_call_target="tpu_custom_call" | custom-call | tf_op jit(solution)/shard_map/step/pallas_call | solution.py:452
  81.6 0.0 copy-start
  81.6 2.2 %copy.16 = f32[3,3,3,64,64]{4,3,2,1,0:T(8,128)} copy(f32[3,3,3,64,64]{4,3,2,1,0:T(8,128)} %bitcast.13) | data formatting | bytes 884736
  83.8 0.0 copy-done
  83.9 0.0 copy-start.1
  83.9 0.7 copy.17
  84.6 0.3 copy-done.1
  84.9 0.7 copy.18
Async XLA Ops:
  81.6 2.2 %copy-start = (f32[512,128]{1,0:T(8,128)S(1)}, f32[512,128]{1,0:T(8,128)}, u32[]{:S(2)}) copy-start(f32[512,128]{1,0:T(8,128)} %get-tuple-element.7) | copy-start | bytes 786436
  83.9 1.0 %copy-start.1 = (f32[128,256]{1,0:T(8,128)S(1)}, f32[128,256]{1,0:T(8,128)}, u32[]{:S(2)}) copy-start(f32[128,256]{1,0:T(8,128)} %get-tuple-element.14) | copy-start | bytes 393220

commit v4 on v3

--- a/solution.py
+++ b/solution.py
@@ -63,7 +63,7 @@
     dx, dy = (x + 8) >> 3, (y + 8) >> 3
     px, py = (n >> 2) + dx - 1, (n & 3) + dy - 1
     side = py * 8 + (y & 7)
-    spot = side + jnp.where(px < 0, 512, jnp.where(px > 1, 544, (x & 7) * 64 + px * 32))
+    spot = side + jnp.where(px < 0, 512, jnp.where(px > 1, 544, (x & 7) * 8 + px * 256 + py * 56))
     linked = ones_where(near >= 0)
     narrow = ones_where(iota((27, 16), 0) == 3 * iota((27, 16), 1) + 1)
     by_row = dot(brick_rows(), dot(linked, narrow).astype(BF))
@@ -84,9 +84,9 @@
 
 
 def step_kernel(
-    nz, ny, src_ref, cot_ref, own_v, own_s, near_ref, occ_ref, w_ref, wd_ref, wp_ref,
-    gwc_ref, gwd_ref, gwp_ref,
-    source, halo_in, pool0, pool1, pool2, pool3, picked, far_in, land0, land1, land2, land3, dec_in, dec_s,
+    nz, ny, feat_any, cot_ref, own_v, near_ref, occ_ref, w_any, wd_any, wp_any,
+    full_ref,
+    feat_ref, w_ref, wd_ref, wp_ref, load_sem, fill_sem, source, halo_out, halo_in, pool0, pool1, pool2, pool3, picked, far_in, land0, land1, land2, land3, dec_in, dec_s,
     taps, pre, occ_at, hid_t, gpre_t, sums, part, cot_here, order_at,
     tosend, arrived, plane_out, plane_in, depth_out, depth_in, full,
     halo_send, halo_recv, dec_send, dec_recv, dec_sem,
@@ -117,9 +117,15 @@
     barrier = pltpu.get_barrier_semaphore()
     for mate in mates_all:
         pl.semaphore_signal(barrier, inc=1, device_id=mate, device_id_type=MESH)
+    fills = []
     for k in range(NSUB):
         quarter = cot_ref.shape[1] // NSUB
-        (pool0, pool1, pool2, pool3)[k][c, z] = cot_ref[:, k * quarter : (k + 1) * quarter, :]
+        home = (pool0, pool1, pool2, pool3)[k].at[c, z]
+        fills.append(pltpu.make_async_copy(cot_ref.at[:, pl.ds(k * quarter, quarter), :], home, fill_sem.at[k]))
+    pairs_in = ((feat_any, feat_ref), (w_any, w_ref), (wd_any, wd_ref), (wp_any, wp_ref))
+    loads = [pltpu.make_async_copy(src, dst, load_sem.at[i]) for i, (src, dst) in enumerate(pairs_in)]
+    for copy in fills + loads:
+        copy.start()
     tgt = tap_targets(near_ref[...])
     pl.semaphore_wait(barrier, len(mates_all))
 
@@ -135,9 +141,6 @@
         pending.append(copy)
         return copy
 
-    rows_src = src_ref.shape[0]
-    halo_up = send(src_ref.at[pl.ds(rows_src - 32, 32)], halo_in.at[0], halo_send.at[0], halo_recv.at[0], ahead)
-    halo_down = send(src_ref.at[pl.ds(0, 32)], halo_in.at[1], halo_send.at[1], halo_recv.at[1], behind)
     dec_copies = [send(own_v, dec_in.at[g], dec_send.at[g], dec_recv.at[g], row[g]) for g in range(NX - 1)]
     cells = cot_ref.shape[1] // NSUB
     rights, lefts, mates, rows = {}, {}, {}, {}
@@ -182,6 +185,7 @@
     fars, nears = {}, {}
 
     def start_rows(k):
+        fills[k].wait()
         for t in range(nz):
             mates[t, k].wait_recv()
         hop = 1 if k % 2 == 0 else NX - 1
@@ -230,22 +234,36 @@
         for copy in local:
             copy.wait()
 
+    def unfold(b):
+        if b == 0:
+            for copy in loads:
+                copy.wait()
+        r, q = iota((512, 1), 0), iota((1, 512), 1)
+        by_z = ones_where(q == ((r & 63) << 3) + (r >> 6))
+        got = dot(by_z, feat_ref[b], 1, 1)
+        blank = jnp.zeros((64, 64), F32)
+        for t in range(5):
+            first = got[128 * t - 64 : 128 * t] if t > 0 else blank
+            second = got[128 * t : 128 * t + 64] if t < 4 else blank
+            tile = jnp.concatenate([first, second], axis=1).astype(BF)
+            source[64 * b : 64 * b + 64, 128 * t : 128 * t + 128] = tile
+
+    halos = []
+
+    def faces():
+        r, q = iota((32, 1), 0), iota((1, 512), 1)
+        base = ((r >> 3) << 6) + (r & 7)
+        for side, start in ((0, 4 * 64 + 56), (1, 0)):
+            halo_out[side] = dot(ones_where(q == base + start), source[0:512]).astype(BF)
+        halos.append(send(halo_out.at[0], halo_in.at[0], halo_send.at[0], halo_recv.at[0], ahead))
+        halos.append(send(halo_out.at[1], halo_in.at[1], halo_send.at[1], halo_recv.at[1], behind))
+        source[512:576] = jnp.zeros((64, 640), BF)
+
     def halo():
-        halo_up.wait_recv()
-        halo_down.wait_recv()
-        low = iota((1, 128), 1) < 64
-
-        def shifted(lo, block):
-            size = block.shape[0]
-            last = jnp.zeros((size, 128), F32)
-            for t in range(5):
-                now = pltpu.roll(block[:, 128 * t : 128 * t + 128].astype(F32), 64, 1) if t < 4 else jnp.zeros((size, 128), F32)
-                source[lo : lo + size, 128 * t : 128 * t + 128] = jnp.where(low, last, now).astype(BF)
-                last = now
-
-        shifted(0, src_ref[...])
-        shifted(512, halo_in[0])
-        shifted(544, halo_in[1])
+        for copy in halos:
+            copy.wait_recv()
+        source[512:544] = halo_in[0]
+        source[544:576] = halo_in[1]
 
     def tap_step(tap):
         spots = iota((1, 576), 1).astype(F32)
@@ -260,7 +278,7 @@
         for t in range(4):
             lanes = slice(128 * t, 128 * t + 128)
             got = dot(moved[:, 128 * t : 128 * t + 256], u)
-            pre[:, lanes] = got if tap == 0 else pre[:, lanes] + got
+            pre[:, lanes] = got if tap == 3 else pre[:, lanes] + got
 
     def hide(ij):
         a = slice(128 * ij, 128 * ij + 128)
@@ -286,13 +304,14 @@
         r = iota((512, 1), 0)
         order_at[...] = ones_where(iota((1, 512), 1) == 4 * (r & 127) + (r >> 7))
 
-    jobs = [asks, halo]
-    jobs += [lambda tap=tap: tap_step(tap) for tap in range(9)]
-    jobs += [occupy]
+    jobs = [lambda b=b: unfold(b) for b in range(8)]
+    jobs += [faces, asks, occupy, ordering]
+    jobs += [lambda tap=tap: tap_step(tap) for tap in (3, 4, 5)]
+    jobs += [halo]
+    jobs += [lambda tap=tap: tap_step(tap) for tap in (0, 1, 2, 6, 7, 8)]
     jobs += [lambda ij=ij: hide(ij) for ij in range(4)]
     jobs += [coarsen]
     jobs += [lambda ij=ij: reslope(ij) for ij in range(4)]
-    jobs += [ordering]
 
     def work():
         if jobs:
@@ -425,42 +444,64 @@
         shares.append(send(home, home, share_send.at[g], share_recv.at[g], pair))
     for copy in shares:
         copy.wait_recv()
+    full_ref[...] = full[...]
+    for copy in pending:
+        copy.wait_send()
+
+
+def unpack_kernel(full_ref, gwc_ref, gwd_ref, gwp_ref):
+    np_ = full_ref.shape[1]
     for j in range(14):
-        chunk = full[j // np_, j % np_].astype(F32)
+        chunk = full_ref[j // np_, j % np_].astype(F32)
         gwc_ref[2 * j] = chunk[:, :64]
         if 2 * j + 1 < 27:
             gwc_ref[2 * j + 1] = pltpu.roll(chunk, 64, 1)[:, :64]
     for j in range(8):
         k = 14 + j
-        gwd_ref[64 * j : 64 * j + 64, :] = full[k // np_, k % np_].astype(F32)
+        gwd_ref[64 * j : 64 * j + 64, :] = full_ref[k // np_, k % np_].astype(F32)
     for j in range(4):
         r, t = j % 2, j // 2
         k = 22 + j
-        gwp_ref[64 * r : 64 * r + 64, 128 * t : 128 * t + 128] = full[k // np_, k % np_].astype(F32)
-    for copy in pending:
-        copy.wait_send()
-
-
-def step(nz, ny, src, cot, owners, near, occ, w, wd, wp):
-    slots, cells, wide = cot.shape
-    chunk = (slots, cells // NSUB, wide)
-    dma = pltpu.SemaphoreType.DMA
+        gwp_ref[64 * r : 64 * r + 64, 128 * t : 128 * t + 128] = full_ref[k // np_, k % np_].astype(F32)
+
+
+def unpack(full):
     vmem = pl.BlockSpec(memory_space=pltpu.VMEM)
-    smem = pl.BlockSpec(memory_space=pltpu.SMEM)
-    far = nz // 2
-    np_ = ny * NX
     return pl.pallas_call(
-        lambda *refs: step_kernel(nz, ny, *refs),
+        unpack_kernel,
         out_shape=(
             jax.ShapeDtypeStruct((27, 64, 64), F32),
             jax.ShapeDtypeStruct((512, 128), F32),
             jax.ShapeDtypeStruct((128, 256), F32),
         ),
-        in_specs=[vmem, vmem, vmem, smem] + [vmem] * 5,
+        in_specs=[vmem],
         out_specs=(vmem,) * 3,
+        name="unpack",
+    )(full)
+
+
+def step(nz, ny, feat, cot, owners, near, occ, w, wd, wp):
+    slots, cells, wide = cot.shape
+    chunk = (slots, cells // NSUB, wide)
+    dma = pltpu.SemaphoreType.DMA
+    vmem = pl.BlockSpec(memory_space=pltpu.VMEM)
+    hbm = pl.BlockSpec(memory_space=pl.ANY)
+    far = nz // 2
+    np_ = ny * NX
+    return pl.pallas_call(
+        lambda *refs: step_kernel(nz, ny, *refs),
+        out_shape=jax.ShapeDtypeStruct((NC, np_, 64, 128), BF),
+        in_specs=[hbm, hbm] + [vmem] * 3 + [hbm] * 3,
+        out_specs=vmem,
         scratch_shapes=[
+            pltpu.VMEM(feat.shape, BF),
+            pltpu.VMEM(w.shape, BF),
+            pltpu.VMEM(wd.shape, BF),
+            pltpu.VMEM(wp.shape, BF),
+            dma((4,)), dma((NSUB,)),
             pltpu.VMEM((576, 640), BF),
-            pltpu.VMEM((2, 32, 512), BF),
+            pltpu.VMEM((2, 32, 640), BF),
+            pltpu.VMEM((2, 32, 640), BF),
             *[pltpu.VMEM((NC, nz) + chunk, BF)] * NSUB,
             pltpu.VMEM((3, NSUB) + chunk, BF),
             pltpu.VMEM((NSUB,) + chunk, BF),
@@ -491,17 +532,17 @@
         ],
         compiler_params=pltpu.CompilerParams(collective_id=0, has_side_effects=True),
         name="step",
-    )(src, cot, owners, owners, near, occ, w, wd, wp)
+    )(feat, cot, owners, near, occ, w, wd, wp)
 
 
 def shards(features, occupancy, neighbours, owners, w_conv, w_down, w_point, cotangent):
     nz = lax.axis_size("brick") // (NX * NC)
     ny = lax.axis_size("dp")
-    flat = features[0].reshape(8, 8, 8, 512).transpose(1, 0, 2, 3).reshape(512, 512)
-    gwc, gwd, gwp = step(
-        nz, ny, flat, cotangent[0], owners, neighbours[0], occupancy[0],
+    full = step(
+        nz, ny, jnp.swapaxes(features[0], 1, 2), cotangent[0], owners, neighbours[0], occupancy[0],
         w_conv.reshape(9, 192, 64), w_down.reshape(512, 128), w_point,
     )
+    gwc, gwd, gwp = unpack(full)
     return gwc.reshape(3, 3, 3, 64, 64), gwd.reshape(2, 2, 2, 64, 128), gwp
 
 

time: 85.7 us -> 79.1 us (0.923)
  local copies, waits for them, and re-layouts: 6.84 us -> 0 us
    unnamed x8 -> x0, local copies, waits for them, and re-layouts: 5.39 us -> none
    pallas_call x1 -> x2, Pallas kernels: 78 us -> 78.3 us  [the longest x1 76.1 us: step(): pl.pallas_call(lambda *refs: step_kernel(nz, ny, *refs), out_shape=jax.Sh...]
where the time goes in v4:
time: 79.1 us; the launch traced here: 78.9 us
  Pallas kernels  78.3 us (99%)
    pallas_call x1, Pallas kernels, step(): pl.pallas_call(lambda *refs: step_kernel(nz, ny, *refs), out_shape=jax.Sh...  76.1 us
    pallas_call x1, Pallas kernels, unpack(): pl.pallas_call(unpack_kernel, out_shape=(jax.ShapeDtypeStruct((27, 64, 64...  2.15 us

profile of v4, /device:TPU:1, one launch (start us, length us, event | category | flops | bytes accessed | tf_op | source)
XLA Modules:
  0.0 78.9 jit_solution(3847667603349462899)
XLA Ops:
  0.6 76.1 %step.1.full_ref = bf16[2,16,64,128]{3,2,1,0:T(8,128)(2,1)} custom-call(bf16[8,64,512]{2,1,0:T(8,128)(2,1)} %bitcast.10, bf16[8,64,256]{2,1,0:T(8,128)(2,1)} %bitcast.12, s32[1,8]{1,0:T(1,128)} %refs_2_.1, s32[8,27]{1,0:T(8,128)} %bitcast.15, s32[8,512]{1,0:T(8,128)} %bitcast.14, bf16[9,192,64]{2,1,0:T(8,128)(2,1)} %bitcast.11, bf16[512,128]{1,0:T(8,128)(2,1)} %bitcast.13, ...), custom_call_target="tpu_custom_call" | custom-call | tf_op jit(solution)/shard_map/step/pallas_call | solution.py:491
  76.8 2.1 %unpack.1 = (f32[27,64,64]{2,1,0:T(8,128)}, f32[512,128]{1,0:T(8,128)}, f32[128,256]{1,0:T(8,128)}) custom-call(bf16[2,16,64,128]{3,2,1,0:T(8,128)(2,1)} %step.1.full_ref), custom_call_target="tpu_custom_call" | custom-call | tf_op jit(solution)/shard_map/unpack/pallas_call | solution.py:470

commit v5 on v4

--- a/solution.py
+++ b/solution.py
@@ -37,9 +37,11 @@
     return lax.dot_general(a, b, (((ca,), (cb,)), ((), ())), preferred_element_type=F32)
 
 
-RIGHT = ((1, 0), (1, 1), (1, 2), (2, 0), (2, 1), (2, 2), (3, 0), (3, 1), (1, 3), (4, 0), (3, 2), (2, 3), (4, 2), (3, 3))
+RIGHT = ((1, 0), (1, 1), (1, 2), (2, 0), (2, 1), (2, 2), (1, 3), (3, 0), (3, 1), (3, 2), (2, 3), (4, 0), (4, 2), (3, 3))
 LEFT = tuple((s, k ^ 1) for s, k in RIGHT)
 LAG = 3
+EARLY = 6
+USED = 13
 
 
 def iota(shape, dim):
@@ -377,12 +379,45 @@
             a = slice(128 * ij, 128 * ij + 128)
             b = slice(128 * r, 128 * r + 128)
             gpre_t[b, a] = (ghid[b, a] * pre[a, b]).astype(BF).T
-    for j in range(8):
-        part[14 + j] = gwd[64 * j : 64 * j + 64, :]
-    for j in range(4):
-        r, t = j % 2, j // 2
-        part[22 + j] = gwp[64 * r : 64 * r + 64, 128 * t : 128 * t + 128]
+    for e in range(12):
+        if e < 8:
+            piece = gwd[64 * e : 64 * e + 64, :]
+        else:
+            r, t = e % 2, (e - 8) // 2
+            piece = gwp[64 * r : 64 * r + 64, 128 * t : 128 * t + 128]
+        part[e // EARLY * np_ + e % EARLY] = piece
+
+    firsts = []
+
+    def share_part(lo, n):
+        i = len(firsts)
+        at_ = pl.ds(lo, n)
+        tosend[at_] = part[pl.ds((1 - c) * np_ + lo, n)].astype(BF)
+        firsts.append(send(tosend.at[at_], arrived.at[at_], pair_send.at[i], pair_recv.at[i], pair))
+
+    def add_part(i, lo, n):
+        firsts[i].wait_recv()
+        at_ = pl.ds(lo, n)
+        plane_out[at_] = (part[pl.ds(c * np_ + lo, n)] + arrived[at_].astype(F32)).astype(BF)
+
+    def later(src, dst, ssem, rsem, mate):
+        return pltpu.make_async_remote_copy(
+            src_ref=src, dst_ref=dst, send_sem=ssem, recv_sem=rsem, device_id=mate, device_id_type=MESH
+        )
+
+    seconds = [
+        later(plane_out.at[k], plane_in.at[g], plane_send.at[g], plane_recv.at[g], mate) for mate, k, g in plane
+    ]
+
+    def start_plane(lo, hi):
+        for (_, k, g), copy in zip(plane, seconds):
+            pl.when((k >= lo) & (k < hi))(copy.start)
+
+    share_part(0, EARLY)
     for tap in range(9):
+        if tap == 4:
+            add_part(0, 0, EARLY)
+            start_plane(0, EARLY)
         total = jnp.zeros((128, 256), F32)
         for t in range(4):
             total += dot(gpre_t[128 * t : 128 * t + 128, :], taps[tap, :, 128 * t : 128 * t + 256])
@@ -401,68 +436,81 @@
             odd = pltpu.roll(b0, 64, 1) + b1
         else:
             odd = jnp.zeros_like(even)
-        part[j] = jnp.where(low, even, odd)
-    for j in range(26, 32):
-        part[j] = jnp.zeros((64, 128), F32)
-
-    pieces = 4
-    size = np_ // pieces
-    firsts = []
-    for i in range(pieces):
-        tosend[pl.ds(i * size, size)] = part[pl.ds((1 - c) * np_ + i * size, size)].astype(BF)
-        at = pl.ds(i * size, size)
-        firsts.append(send(tosend.at[at], arrived.at[at], pair_send.at[i], pair_recv.at[i], pair))
-    for i in range(pieces):
-        firsts[i].wait_recv()
-        at = pl.ds(i * size, size)
-        plane_out[at] = (part[pl.ds(c * np_ + i * size, size)] + arrived[at].astype(F32)).astype(BF)
-    seconds = [
-        send(plane_out.at[k], plane_in.at[g], plane_send.at[g], plane_recv.at[g], mate) for mate, k, g in plane
+        part[j // 7 * np_ + EARLY + j % 7] = jnp.where(low, even, odd)
+    share_part(EARLY, 4)
+    share_part(EARLY + 4, USED - EARLY - 4)
+    add_part(1, EARLY, 4)
+    start_plane(EARLY, EARLY + 4)
+    add_part(2, EARLY + 4, USED - EARLY - 4)
+    start_plane(EARLY + 4, USED)
+
+    mine = full.at[c, me]
+    thirds = [
+        later(depth_out, depth_in.at[z], depth_send.at[g], depth_recv.at[g], mate) for g, mate in enumerate(depth)
     ]
-    total = plane_out[me].astype(F32)
+    backs = [later(mine, mine, back_send.at[g], back_recv.at[g], mate) for mate, k, g in plane]
+    first_share = later(mine, mine, share_send.at[0], share_recv.at[0], pair)
+
+    @pl.when(me < USED)
+    def _():
+        total = plane_out[me].astype(F32)
+        for g in range(1, np_):
+            seconds[g - 1].wait_recv()
+            total += plane_in[g].astype(F32)
+        depth_out[...] = total.astype(BF)
+        for copy in thirds:
+            copy.start()
+        depth_in[z] = total.astype(BF)
+        for copy in thirds:
+            copy.wait_recv()
+        total = depth_in[0].astype(F32)
+        for k in range(1, nz):
+            total += depth_in[k].astype(F32)
+        full[c, me] = total.astype(BF)
+        for copy in backs:
+            copy.start()
+        first_share.start()
+
+    shares = []
     for g in range(1, np_):
-        seconds[g - 1].wait_recv()
-        total += plane_in[g].astype(F32)
-    depth_out[...] = total.astype(BF)
-    thirds = [
-        send(depth_out, depth_in.at[z], depth_send.at[g], depth_recv.at[g], mate) for g, mate in enumerate(depth)
-    ]
-    depth_in[z] = total.astype(BF)
-    for copy in thirds:
-        copy.wait_recv()
-    total = depth_in[0].astype(F32)
-    for k in range(1, nz):
-        total += depth_in[k].astype(F32)
-    mine = full.at[c, me]
-    full[c, me] = total.astype(BF)
-    backs = [send(mine, mine, back_send.at[g], back_recv.at[g], mate) for mate, k, g in plane]
-    shares = [send(mine, mine, share_send.at[0], share_recv.at[0], pair)]
-    for g in range(1, np_):
-        backs[g - 1].wait_recv()
-        yy, xx = (y + ny - g // NX) % ny, (x + NX - g % NX) % NX
-        home = full.at[c, yy * NX + xx]
-        shares.append(send(home, home, share_send.at[g], share_recv.at[g], pair))
-    for copy in shares:
-        copy.wait_recv()
-    full_ref[...] = full[...]
+        k = (y + ny - g // NX) % ny * NX + (x + NX - g % NX) % NX
+        home = full.at[c, k]
+        share = later(home, home, share_send.at[g], share_recv.at[g], pair)
+        shares.append((k, share))
+
+        @pl.when(k < USED)
+        def _(g=g, share=share):
+            backs[g - 1].wait_recv()
+            share.start()
+
+    for k, share in [(me, first_share)] + shares:
+        pl.when(k < USED)(share.wait)
+    full_ref[...] = full[:, :USED]
+
+    @pl.when(me < USED)
+    def _():
+        for copy in thirds + backs:
+            copy.wait_send()
+
+    for (_, k, g), copy in zip(plane, seconds):
+        pl.when(k < USED)(copy.wait_send)
     for copy in pending:
         copy.wait_send()
 
 
 def unpack_kernel(full_ref, gwc_ref, gwd_ref, gwp_ref):
-    np_ = full_ref.shape[1]
     for j in range(14):
-        chunk = full_ref[j // np_, j % np_].astype(F32)
+        chunk = full_ref[j // 7, EARLY + j % 7].astype(F32)
         gwc_ref[2 * j] = chunk[:, :64]
         if 2 * j + 1 < 27:
             gwc_ref[2 * j + 1] = pltpu.roll(chunk, 64, 1)[:, :64]
-    for j in range(8):
-        k = 14 + j
-        gwd_ref[64 * j : 64 * j + 64, :] = full_ref[k // np_, k % np_].astype(F32)
-    for j in range(4):
-        r, t = j % 2, j // 2
-        k = 22 + j
-        gwp_ref[64 * r : 64 * r + 64, 128 * t : 128 * t + 128] = full_ref[k // np_, k % np_].astype(F32)
+    for e in range(12):
+        chunk = full_ref[e // EARLY, e % EARLY].astype(F32)
+        if e < 8:
+            gwd_ref[64 * e : 64 * e + 64, :] = chunk
+        else:
+            r, t = e % 2, (e - 8) // 2
+            gwp_ref[64 * r : 64 * r + 64, 128 * t : 128 * t + 128] = chunk
 
 
 def unpack(full):
@@ -490,7 +538,7 @@
     np_ = ny * NX
     return pl.pallas_call(
         lambda *refs: step_kernel(nz, ny, *refs),
-        out_shape=jax.ShapeDtypeStruct((NC, np_, 64, 128), BF),
+        out_shape=jax.ShapeDtypeStruct((NC, USED, 64, 128), BF),
         in_specs=[hbm, hbm] + [vmem] * 3 + [hbm] * 3,
         out_specs=vmem,
         scratch_shapes=[

time: 79.1 us -> 75.8 us (0.958)
  Pallas kernels: 78.3 us -> 75 us
    pallas_call x1, Pallas kernels: 76.1 us -> 72.8 us  [step(): pl.pallas_call(lambda *refs: step_kernel(nz, ny, *refs), out_shape=jax.Sh...]
where the time goes in v5:
time: 75.8 us; the launch traced here: 75.6 us
  Pallas kernels  75 us (99%)
    pallas_call x1, Pallas kernels, step(): pl.pallas_call(lambda *refs: step_kernel(nz, ny, *refs), out_shape=jax.Sh...  72.8 us
    pallas_call x1, Pallas kernels, unpack(): pl.pallas_call(unpack_kernel, out_shape=(jax.ShapeDtypeStruct((27, 64, 64...  2.11 us

profile of v5, /device:TPU:1, one launch (start us, length us, event | category | flops | bytes accessed | tf_op | source)
XLA Modules:
  0.0 75.6 jit_solution(10373295253507987610)
XLA Ops:
  0.6 72.8 %step.1.full_ref = bf16[2,13,64,128]{3,2,1,0:T(8,128)(2,1)} custom-call(bf16[8,64,512]{2,1,0:T(8,128)(2,1)} %bitcast.10, bf16[8,64,256]{2,1,0:T(8,128)(2,1)} %bitcast.12, s32[1,8]{1,0:T(1,128)} %refs_2_.1, s32[8,27]{1,0:T(8,128)} %bitcast.15, s32[8,512]{1,0:T(8,128)} %bitcast.14, bf16[9,192,64]{2,1,0:T(8,128)(2,1)} %bitcast.11, bf16[512,128]{1,0:T(8,128)(2,1)} %bitcast.13, ...), custom_call_target="tpu_custom_call" | custom-call | tf_op jit(solution)/shard_map/step/pallas_call | solution.py:539
  73.5 2.1 %unpack.1 = (f32[27,64,64]{2,1,0:T(8,128)}, f32[512,128]{1,0:T(8,128)}, f32[128,256]{1,0:T(8,128)}) custom-call(bf16[2,13,64,128]{3,2,1,0:T(8,128)(2,1)} %step.1.full_ref), custom_call_target="tpu_custom_call" | custom-call | tf_op jit(solution)/shard_map/unpack/pallas_call | solution.py:518

commit v6 on v5

--- a/solution.py
+++ b/solution.py
@@ -343,8 +343,7 @@
                 waiting.append((i, k))
         if i == 2:
             ready()
-        if i >= 3:
-            work()
+        if i >= 2:
             work()
         while waiting and waiting[0][0] < i:
             k = waiting.pop(0)[1]

time: 75.8 us -> 74.7 us (0.985)
  Pallas kernels: 75 us -> 73.9 us
    pallas_call x1, Pallas kernels: 72.8 us -> 71.8 us  [step(): pl.pallas_call(lambda *refs: step_kernel(nz, ny, *refs), out_shape=jax.Sh...]
where the time goes in v6:
time: 74.7 us; the launch traced here: 74.5 us
  Pallas kernels  73.9 us (99%)
    pallas_call x1, Pallas kernels, step(): pl.pallas_call(lambda *refs: step_kernel(nz, ny, *refs), out_shape=jax.Sh...  71.8 us
    pallas_call x1, Pallas kernels, unpack(): pl.pallas_call(unpack_kernel, out_shape=(jax.ShapeDtypeStruct((27, 64, 64...  2.11 us

profile of v6, /device:TPU:1, one launch (start us, length us, event | category | flops | bytes accessed | tf_op | source)
XLA Modules:
  0.0 74.5 jit_solution(10227999911067331790)
XLA Ops:
  0.6 71.8 %step.1.full_ref = bf16[2,13,64,128]{3,2,1,0:T(8,128)(2,1)} custom-call(bf16[8,64,512]{2,1,0:T(8,128)(2,1)} %bitcast.10, bf16[8,64,256]{2,1,0:T(8,128)(2,1)} %bitcast.12, s32[1,8]{1,0:T(1,128)} %refs_2_.1, s32[8,27]{1,0:T(8,128)} %bitcast.15, s32[8,512]{1,0:T(8,128)} %bitcast.14, bf16[9,192,64]{2,1,0:T(8,128)(2,1)} %bitcast.11, bf16[512,128]{1,0:T(8,128)(2,1)} %bitcast.13, ...), custom_call_target="tpu_custom_call" | custom-call | tf_op jit(solution)/shard_map/step/pallas_call | solution.py:538
  72.4 2.1 %unpack.1 = (f32[27,64,64]{2,1,0:T(8,128)}, f32[512,128]{1,0:T(8,128)}, f32[128,256]{1,0:T(8,128)}) custom-call(bf16[2,13,64,128]{3,2,1,0:T(8,128)(2,1)} %step.1.full_ref), custom_call_target="tpu_custom_call" | custom-call | tf_op jit(solution)/shard_map/unpack/pallas_call | solution.py:517

commit v7 on v6

--- a/solution.py
+++ b/solution.py
@@ -18,6 +18,10 @@
 def where_am_i():
     spot = lax.axis_index("brick")
     return spot // (NX * NC), spot // NC % NX, spot % NC
+
+
+def hops(step, size):
+    return min(step, size - step)
 
 
 def brick_at(z, x, c):
@@ -111,10 +115,10 @@
     row = [at(y, brick_at(z, (x + g) % NX, c)) for g in range(1, NX)]
     ahead, behind = at(y, (spot + 1) % many), at(y, (spot + many - 1) % many)
     plane = []
-    for g in range(1, np_):
+    for g in sorted(range(1, np_), key=lambda g: -hops(g // NX, ny) - hops(g % NX, NX)):
         yy, xx = (y + g // NX) % ny, (x + g % NX) % NX
         plane.append((at(yy, brick_at(z, xx, c)), yy * NX + xx, g))
-    depth = [at(y, brick_at((z + g) % nz, x, c)) for g in range(1, nz)]
+    depth = [at(y, brick_at((z + g) % nz, x, c)) for g in sorted(range(1, nz), key=lambda g: -hops(g, nz))]
     mates_all = [pair, ahead, behind] + [p[0] for p in plane] + depth
     barrier = pltpu.get_barrier_semaphore()
     for mate in mates_all:
@@ -404,13 +408,13 @@
             src_ref=src, dst_ref=dst, send_sem=ssem, recv_sem=rsem, device_id=mate, device_id_type=MESH
         )
 
-    seconds = [
-        later(plane_out.at[k], plane_in.at[g], plane_send.at[g], plane_recv.at[g], mate) for mate, k, g in plane
-    ]
+    seconds = {
+        g: later(plane_out.at[k], plane_in.at[g], plane_send.at[g], plane_recv.at[g], mate) for mate, k, g in plane
+    }
 
     def start_plane(lo, hi):
-        for (_, k, g), copy in zip(plane, seconds):
-            pl.when((k >= lo) & (k < hi))(copy.start)
+        for _, k, g in plane:
+            pl.when((k >= lo) & (k < hi))(seconds[g].start)
 
     share_part(0, EARLY)
     for tap in range(9):
@@ -447,14 +451,14 @@
     thirds = [
         later(depth_out, depth_in.at[z], depth_send.at[g], depth_recv.at[g], mate) for g, mate in enumerate(depth)
     ]
-    backs = [later(mine, mine, back_send.at[g], back_recv.at[g], mate) for mate, k, g in plane]
+    backs = {g: later(mine, mine, back_send.at[g], back_recv.at[g], mate) for mate, k, g in plane}
     first_share = later(mine, mine, share_send.at[0], share_recv.at[0], pair)
 
     @pl.when(me < USED)
     def _():
         total = plane_out[me].astype(F32)
         for g in range(1, np_):
-            seconds[g - 1].wait_recv()
+            seconds[g].wait_recv()
             total += plane_in[g].astype(F32)
         depth_out[...] = total.astype(BF)
         for copy in thirds:
@@ -466,7 +470,7 @@
         for k in range(1, nz):
             total += depth_in[k].astype(F32)
         full[c, me] = total.astype(BF)
-        for copy in backs:
+        for copy in backs.values():
             copy.start()
         first_share.start()
 
@@ -479,7 +483,7 @@
 
         @pl.when(k < USED)
         def _(g=g, share=share):
-            backs[g - 1].wait_recv()
+            backs[g].wait_recv()
             share.start()
 
     for k, share in [(me, first_share)] + shares:
@@ -488,11 +492,11 @@
 
     @pl.when(me < USED)
     def _():
-        for copy in thirds + backs:
+        for copy in thirds + list(backs.values()):
             copy.wait_send()
 
-    for (_, k, g), copy in zip(plane, seconds):
-        pl.when(k < USED)(copy.wait_send)
+    for _, k, g in plane:
+        pl.when(k < USED)(seconds[g].wait_send)
     for copy in pending:
         copy.wait_send()
 

time: 74.7 us -> 73.9 us (0.989)
  Pallas kernels: 73.9 us -> 73 us
    pallas_call x1, Pallas kernels: 71.8 us -> 70.9 us  [step(): pl.pallas_call(lambda *refs: step_kernel(nz, ny, *refs), out_shape=jax.Sh...]
where the time goes in v7:
time: 73.9 us; the launch traced here: 73.7 us
  Pallas kernels  73 us (99%)
    pallas_call x1, Pallas kernels, step(): pl.pallas_call(lambda *refs: step_kernel(nz, ny, *refs), out_shape=jax.Sh...  70.9 us
    pallas_call x1, Pallas kernels, unpack(): pl.pallas_call(unpack_kernel, out_shape=(jax.ShapeDtypeStruct((27, 64, 64...  2.11 us

profile of v7, /device:TPU:1, one launch (start us, length us, event | category | flops | bytes accessed | tf_op | source)
XLA Modules:
  0.0 73.7 jit_solution(13223389205205604748)
XLA Ops:
  0.6 70.9 %step.1.full_ref = bf16[2,13,64,128]{3,2,1,0:T(8,128)(2,1)} custom-call(bf16[8,64,512]{2,1,0:T(8,128)(2,1)} %bitcast.10, bf16[8,64,256]{2,1,0:T(8,128)(2,1)} %bitcast.12, s32[1,8]{1,0:T(1,128)} %refs_2_.1, s32[8,27]{1,0:T(8,128)} %bitcast.15, s32[8,512]{1,0:T(8,128)} %bitcast.14, bf16[9,192,64]{2,1,0:T(8,128)(2,1)} %bitcast.11, bf16[512,128]{1,0:T(8,128)(2,1)} %bitcast.13, ...), custom_call_target="tpu_custom_call" | custom-call | tf_op jit(solution)/shard_map/step/pallas_call | solution.py:542
  71.6 2.1 %unpack.1 = (f32[27,64,64]{2,1,0:T(8,128)}, f32[512,128]{1,0:T(8,128)}, f32[128,256]{1,0:T(8,128)}) custom-call(bf16[2,13,64,128]{3,2,1,0:T(8,128)(2,1)} %step.1.full_ref), custom_call_target="tpu_custom_call" | custom-call | tf_op jit(solution)/shard_map/unpack/pallas_call | solution.py:521

commit v8 on v7

--- a/solution.py
+++ b/solution.py
@@ -11,6 +11,7 @@
 NC = 2
 NSUB = 4
 NB = 8
+HALF = 4
 BF = jnp.bfloat16
 F32 = jnp.float32
 
@@ -195,9 +196,14 @@
         for t in range(nz):
             mates[t, k].wait_recv()
         hop = 1 if k % 2 == 0 else NX - 1
-        for b in range(NB):
-            picked[0, k, b] = pick(NX - 1 - NX // 2, k, b)
-        fars[k] = send(picked.at[0, k], far_in.at[k], row_send.at[0, k], row_recv.at[0, k], row[hop - 1])
+        for h in range(2):
+            for b in range(HALF * h, HALF * h + HALF):
+                picked[0, k, b] = pick(NX - 1 - NX // 2, k, b)
+            part_of = pl.ds(HALF * h, HALF)
+            i = 3 * h
+            fars[k, h] = send(
+                picked.at[0, k, part_of], far_in.at[k, part_of], row_send.at[i, k], row_recv.at[i, k], row[hop - 1]
+            )
         back = NX - hop
         for b in range(NB):
             picked[1, k, b] = pick(NX - 1 - back, k, b)
@@ -206,16 +212,22 @@
             lands[k][0, b] = pick(NX - 1, k, b)
 
     def relay(k):
-        fars[k].wait_recv()
         hop = 1 if k % 2 == 0 else NX - 1
         g = NX - 1 - hop
-        for b in range(NB):
-            mine = dec_s[g, 0, b] // (NB * NC) % NX == x
-            picked[2, k, b] = jnp.where(mine, pick(g, k, b).astype(F32), far_in[k, b].astype(F32)).astype(BF)
-        rows[k] = send(picked.at[2, k], lands[k].at[1], row_send.at[2, k], row_recv.at[2, k], row[hop - 1])
+        for h in range(2):
+            fars[k, h].wait_recv()
+            for b in range(HALF * h, HALF * h + HALF):
+                mine = dec_s[g, 0, b] // (NB * NC) % NX == x
+                picked[2, k, b] = jnp.where(mine, pick(g, k, b).astype(F32), far_in[k, b].astype(F32)).astype(BF)
+            part_of = pl.ds(HALF * h, HALF)
+            i = 2 + 2 * h
+            rows[k, h] = send(
+                picked.at[2, k, part_of], lands[k].at[1, part_of], row_send.at[i, k], row_recv.at[i, k], row[hop - 1]
+            )
 
     def finish(k):
-        rows[k].wait_recv()
+        rows[k, 0].wait_recv()
+        rows[k, 1].wait_recv()
         nears[k].wait_recv()
         behind_x = (x + NX - 1) % NX if k % 2 == 1 else (x + 1) % NX
         for b in range(NB):
@@ -577,7 +589,7 @@
             pltpu.VMEM((NC, np_, 64, 128), BF),
             dma((2,)), dma((2,)), dma((NX - 1,)), dma((NX - 1,)), dma((NX,)),
             dma((far, NSUB)), dma((far, NSUB)), dma((far, NSUB)), dma((far, NSUB)),
-            dma((nz, NSUB)), dma((nz, NSUB)), dma((NX - 1, NSUB)), dma((NX - 1, NSUB)),
+            dma((nz, NSUB)), dma((nz, NSUB)), dma((NX + 1, NSUB)), dma((NX + 1, NSUB)),
             dma((4,)), dma((4,)), dma((np_,)), dma((np_,)), dma((nz,)), dma((nz,)),
             dma((np_,)), dma((np_,)), dma((np_,)), dma((np_,)),
         ],

time: 73.9 us -> 73.9 us (level)
  no operation moved by 1% of the time
where the time goes in v8:
time: 73.9 us; the launch traced here: 73.8 us
  Pallas kernels  73.1 us (99%)
    pallas_call x1, Pallas kernels, step(): pl.pallas_call(lambda *refs: step_kernel(nz, ny, *refs), out_shape=jax.Sh...  71 us
    pallas_call x1, Pallas kernels, unpack(): pl.pallas_call(unpack_kernel, out_shape=(jax.ShapeDtypeStruct((27, 64, 64...  2.11 us

profile of v8, /device:TPU:1, one launch (start us, length us, event | category | flops | bytes accessed | tf_op | source)
XLA Modules:
  0.0 73.8 jit_solution(11288865852243155200)
XLA Ops:
  0.6 71.0 %step.1.full_ref = bf16[2,13,64,128]{3,2,1,0:T(8,128)(2,1)} custom-call(bf16[8,64,512]{2,1,0:T(8,128)(2,1)} %bitcast.10, bf16[8,64,256]{2,1,0:T(8,128)(2,1)} %bitcast.12, s32[1,8]{1,0:T(1,128)} %refs_2_.1, s32[8,27]{1,0:T(8,128)} %bitcast.15, s32[8,512]{1,0:T(8,128)} %bitcast.14, bf16[9,192,64]{2,1,0:T(8,128)(2,1)} %bitcast.11, bf16[512,128]{1,0:T(8,128)(2,1)} %bitcast.13, ...), custom_call_target="tpu_custom_call" | custom-call | tf_op jit(solution)/shard_map/step/pallas_call | solution.py:554
  71.7 2.1 %unpack.1 = (f32[27,64,64]{2,1,0:T(8,128)}, f32[512,128]{1,0:T(8,128)}, f32[128,256]{1,0:T(8,128)}) custom-call(bf16[2,13,64,128]{3,2,1,0:T(8,128)(2,1)} %step.1.full_ref), custom_call_target="tpu_custom_call" | custom-call | tf_op jit(solution)/shard_map/unpack/pallas_call | solution.py:533
